TPU v7x, 256 devices: a whole 4x4x8 slice. The times are simulated.
256 devices in a mesh: gx: 64 (over z, y, core), gy: 4 (over x).
Axes of the slice: x: 4, y: 4, z: 8, core: 2. Of those that a mesh axis runs over, the one named last changes fastest.
Arguments:
- courant: float32 [512, 512, 256], P('gx', 'gy'), may hold values from 0.05 to 0.2
- first_moment: float32 [512, 512, 256], P('gx', 'gy'), may hold values from -6 to 6
- second_moment: float32 [512, 512, 256], P('gx', 'gy'), may hold values from 0.01 to 1
- adjoint_prev: float32 [512, 512, 256], P('gx', 'gy'), may hold values from -6 to 6
- adjoint_now: float32 [512, 512, 256], P('gx', 'gy'), may hold values from -6 to 6
- forward_field: bfloat16 [4, 512, 512, 256], P(None, 'gx', 'gy'), may hold values from -6 to 6
- traces: float32 [4, 8192, 128], P('gy', 'gx'), may hold values from -6 to 6
- trace_slab: int32 [4, 8192, 1], P('gy', 'gx'), may hold values from 0 to 63; in each aligned block of 128 rows (0 to 127, 128 to 255, ..., all dimensions but the last counted through in order) at most 4 rows name the same one
- trace_cell: int32 [4, 8192], P('gy', 'gx'), may hold values from 0 to 1023
- trace_shot: int32 [4, 8192], P('gy', 'gx'), may hold values from 0 to 15
- rollback: int32 [16], replicated, may hold values 0 or 1
Outputs:
- courant_next: float32 [512, 512, 256], P('gx', 'gy')
- first_next: float32 [512, 512, 256], P('gx', 'gy')
- second_next: float32 [512, 512, 256], P('gx', 'gy')
- adjoint_last: float32 [512, 512, 256], P('gx', 'gy')
Inputs may be any that keep to these rules, and one draw needn't show every extreme that they name: `trace_slab`: within the 128 blocks of one device no x-slab is named by more than 4 blocks; in some devices one x-slab is named by exactly 4.
All inputs are finite; a program needn't handle non-finite values.
Results may differ from a plain program's by a relative error of at most 0.0003.
Values sent between devices are 32-bit elements; how exact they have to be, the bound alone decides.
A program may use at most 64 MiB of HBM per device.

v0:
```python
import math

import jax
import jax.numpy as jnp
from jax import lax
from jax.sharding import PartitionSpec as P

ADJOINT_STEPS = 4
SAMPLES_PER_STEP = 32
ZREC = 8
SHOTS = 16


coefficients = (8.0 / 5.0, -1.0 / 5.0, 8.0 / 315.0, -1.0 / 560.0)
center_weight = -205.0 / 72.0
smooth_length = 4096.0
cosh_value = 1.0 + 0.5 / smooth_length
theta = math.log(cosh_value + math.sqrt(cosh_value * cosh_value - 1.0))
image_gain = 10.0
beta_first = 0.9
beta_second = 0.999
bias_first = 1.0 - 0.9**10
bias_second = 1.0 - 0.999**10
learning_rate = 0.01
epsilon = 1e-08


def padded_2(array, sides, width):
    edges = {}
    for axis, dim in sides:
        peers, length = (lax.axis_size(axis), array.shape[dim])
        up = [(i, (i + 1) % peers) for i in range(peers - 1)]
        last = lax.slice_in_dim(array, length - width, length, axis=dim)
        first = lax.slice_in_dim(array, 0, width, axis=dim)
        edges[dim] = (
            lax.ppermute(last, axis, up),
            lax.ppermute(first, axis, [(b, a) for a, b in up]),
        )
    done = []
    for _, dim in sides:
        low, high = edges[dim]
        around = [(width, width) if d in done else (0, 0) for d in range(array.ndim)]
        array = jnp.concatenate([jnp.pad(low, around), array, jnp.pad(high, around)], axis=dim)
        done.append(dim)
    return array


def sent_together(arrays, axis, split_dim, concat_dim, along):
    widths = [math.prod(a.shape[along:]) for a in arrays]
    both = jnp.concatenate(
        [a.reshape(*a.shape[:along], w) for a, w in zip(arrays, widths)], axis=along
    )
    out = lax.all_to_all(both, axis, split_axis=split_dim, concat_axis=concat_dim, tiled=True)
    parts = jnp.split(out, [sum(widths[:k]) for k in range(1, len(widths))], axis=along)
    return tuple((b.reshape(*out.shape[:along], *a.shape[along:]) for a, b in zip(arrays, parts)))


def smoother(count):
    position = jnp.arange(count, dtype=jnp.int32).astype(jnp.float32)
    lower = jnp.minimum(position[:, None], position[None, :])
    upper = jnp.maximum(position[:, None], position[None, :])
    spread = jnp.abs(position[:, None] - position[None, :])
    numerator = (
        jnp.exp(-theta * spread)
        * (1.0 - jnp.exp(-2.0 * theta * (lower + 1.0)))
        * (1.0 - jnp.exp(-2.0 * theta * (count - upper)))
    )
    denominator = (
        2.0 * smooth_length * math.sinh(theta) * (1.0 - math.exp(-2.0 * theta * (count + 1)))
    )
    return numerator / denominator


def stencil_sum(padded, wavefield):
    length_x, length_y, length_z = wavefield.shape
    summed = 3.0 * center_weight * wavefield
    for offset, weight in enumerate(coefficients, 1):
        paired = padded[4 + offset : 4 + offset + length_x, 4 : 4 + length_y, 4 : 4 + length_z]
        paired = (
            paired + padded[4 - offset : 4 - offset + length_x, 4 : 4 + length_y, 4 : 4 + length_z]
        )
        paired = (
            paired + padded[4 : 4 + length_x, 4 + offset : 4 + offset + length_y, 4 : 4 + length_z]
        )
        paired = (
            paired + padded[4 : 4 + length_x, 4 - offset : 4 - offset + length_y, 4 : 4 + length_z]
        )
        paired = (
            paired + padded[4 : 4 + length_x, 4 : 4 + length_y, 4 + offset : 4 + offset + length_z]
        )
        paired = (
            paired + padded[4 : 4 + length_x, 4 : 4 + length_y, 4 - offset : 4 - offset + length_z]
        )
        summed = summed + weight * paired
    return summed


def laplacian(wavefield):
    padded = padded_2(wavefield, (("gx", 0), ("gy", 1)), 4)
    padded = jnp.pad(padded, ((0, 0), (0, 0), (4, 4)))
    return stencil_sum(padded, wavefield)


def route_traces(traces, trace_slab, trace_cell, trace_shot, rollback, length_x, length_y):
    count_of_slabs = lax.axis_size("gx")
    blocks = traces.shape[1]
    route_limit = max(2, 2 * blocks // count_of_slabs)
    samples = traces[0]
    slabs = trace_slab[0, :, 0]
    cells = trace_cell[0]
    shot_table = trace_shot[0][:, None] == jnp.arange(SHOTS, dtype=jnp.int32)[None, :]
    active_mask = jnp.any(shot_table & (rollback == 0)[None, :], axis=1).astype(jnp.float32)
    slab_table = (slabs[:, None] == jnp.arange(count_of_slabs, dtype=jnp.int32)[None, :]).astype(
        jnp.int32
    )
    earlier = jnp.cumsum(slab_table, axis=0) - slab_table
    slot_index = jnp.sum(earlier * slab_table, axis=1)
    target = slabs * route_limit + slot_index
    placement = (
        target[:, None] == jnp.arange(count_of_slabs * route_limit, dtype=jnp.int32)[None, :]
    )
    cells_sent = (
        jnp.sum(jnp.where(placement, cells[:, None], 0), axis=0)
        .astype(jnp.float32)
        .reshape(count_of_slabs, route_limit)
    )
    placement = placement.astype(jnp.float32)
    masked = samples * active_mask[:, None]
    reduced = masked.reshape(blocks, ADJOINT_STEPS, SAMPLES_PER_STEP).sum(axis=-1)
    packed = jnp.dot(
        placement.T, reduced, precision=lax.Precision.HIGHEST, preferred_element_type=jnp.float32
    ).reshape(count_of_slabs, route_limit, ADJOINT_STEPS)
    traces_landed, cells_got = sent_together((packed, cells_sent), "gx", 0, 0, 2)
    thinned_traces = traces_landed.reshape(count_of_slabs * route_limit, ADJOINT_STEPS)
    cell_ids = cells_got.reshape(-1).astype(jnp.int32)
    cell_table = (
        cell_ids[:, None] == jnp.arange(length_x * length_y, dtype=jnp.int32)[None, :]
    ).astype(jnp.float32)
    source = jnp.dot(
        thinned_traces.T,
        cell_table,
        precision=lax.Precision.HIGHEST,
        preferred_element_type=jnp.float32,
    )
    return source.reshape(ADJOINT_STEPS, length_x, length_y)


def shards(
    courant,
    first_moment,
    second_moment,
    adjoint_prev,
    adjoint_now,
    forward_field,
    traces,
    trace_slab,
    trace_cell,
    trace_shot,
    rollback,
):
    length_x, length_y, length_z = courant.shape
    source = route_traces(traces, trace_slab, trace_cell, trace_shot, rollback, length_x, length_y)
    previous = adjoint_prev
    current = adjoint_now
    image = jnp.zeros(courant.shape, jnp.float32)
    for step_index in range(ADJOINT_STEPS):
        following = 2.0 * current - previous + courant * laplacian(current)
        following = following.at[:, :, ZREC].add(source[step_index])
        image = image + forward_field[step_index].astype(jnp.float32) * following
        previous, current = (current, following)
    gradient = image_gain * image
    line_count = length_x * lax.axis_size("gx")
    table = smoother(line_count)
    lines = lax.all_to_all(gradient, "gx", split_axis=1, concat_axis=0, tiled=True)
    result = jnp.dot(
        table,
        lines.reshape(line_count, -1),
        precision=lax.Precision.HIGHEST,
        preferred_element_type=jnp.float32,
    ).reshape(lines.shape)
    smoothed = lax.all_to_all(result, "gx", split_axis=0, concat_axis=1, tiled=True)
    first_next = beta_first * first_moment + (1.0 - beta_first) * smoothed
    second_next = beta_second * second_moment + (1.0 - beta_second) * smoothed * smoothed
    courant_next = courant - learning_rate * (first_next / bias_first) / (
        jnp.sqrt(second_next / bias_second) + epsilon
    )
    return (courant_next, first_next, second_next, current)


def solution(mesh):
    in_specs = (
        P("gx", "gy", None),
        P("gx", "gy", None),
        P("gx", "gy", None),
        P("gx", "gy", None),
        P("gx", "gy", None),
        P(None, "gx", "gy", None),
        P("gy", "gx", None),
        P("gy", "gx", None),
        P("gy", "gx"),
        P("gy", "gx"),
        P(),
    )
    out_specs = (P("gx", "gy", None), P("gx", "gy", None), P("gx", "gy", None), P("gx", "gy", None))
    return jax.shard_map(shards, mesh=mesh, in_specs=in_specs, out_specs=out_specs, check_vma=False)
```

profile of v0, /device:TPU:1, one launch (start us, length us, event | category | flops | bytes accessed | tf_op | source)
XLA Modules:
  0.0 212.1 jit_solution(16479286634700440162)
XLA Ops:
  0.7 1.4 fusion.182
  2.1 4.6 %collective-permute-start.1 = (f32[4,128,256]{2,1,0:T(8,128)S(1)}, f32[4,128,256]{2,1,0:T(8,128)S(1)}, u32[]{:S(2)}, u32[]{:S(2)}) collective-permute-start(f32[4,128,256]{2,1,0:T(8,128)S(1)} %get-tuple-element.83), channel_id=1, source_target_pairs={{0,4},{4,8},{8,12},{12,16},{16,20},{20,24},{24,28},{28,32},{32,36}... | collective-permute-start | bytes 1572872 | tf_op jit(solution)/shard_map/ppermute | solution.py:36
  6.7 1.9 collective-permute-start
  11.4 12.9 %all-to-all-start = ((f32[64,4,5]{2,1,0:T(4,128)}), f32[64,4,5]{2,1,0:T(4,128)S(1)}, u32[]{:S(2)}, u32[]{:S(2)}) async-start(f32[64,4,5]{2,1,0:T(4,128)} %copy.79), calls=%async_computation | async-start | bytes 262144 | tf_op jit(solution)/shard_map/all_to_all | solution.py:53
  24.4 1.3 collective-permute-start.2
  25.7 4.0 %collective-permute-start.3 = (f32[8,4,256]{2,1,0:T(4,128)S(1)}, f32[8,4,256]{2,1,0:T(4,128)S(1)}, u32[]{:S(2)}, u32[]{:S(2)}) collective-permute-start(f32[8,4,256]{2,1,0:T(4,128)S(1)} %get-tuple-element.81), channel_id=1, source_target_pairs={{0,1},{1,2},{2,3},{4,5},{5,6},{6,7},{8,9},{9,10},{10,11},{12,13},{... | collective-permute-start | bytes 98312 | tf_op jit(solution)/shard_map/ppermute | solution.py:36
  29.7 5.8 %all-to-all-done = f32[64,4,5]{2,1,0:T(4,128)S(1)} async-done(((f32[64,4,5]{2,1,0:T(4,128)}), f32[64,4,5]{2,1,0:T(4,128)S(1)}, u32[]{:S(2)}, u32[]{:S(2)}) %all-to-all-start) | async-done | bytes 5152 | tf_op jit(solution)/shard_map/all_to_all | solution.py:53
  35.4 1.2 fusion.160
  37.3 1.0 copy.81
  39.0 1.1 select_maximum_fusion.12
  40.5 3.3 %fusion.100 = f32[8,128,256]{2,1,0:T(8,128)S(1)} fusion(f32[8,128,256]{2,1,0:T(8,128)S(1)} %copy-done, f32[16,128,256]{2,1,0:T(8,128)S(1)} %get-tuple-element.85, f32[16,4,256]{2,1,0:T(4,128)S(1)} %pad.47, f32[16,4,256]{2,1,0:T(4,128)S(1)} %pad.46, f32[16,136,264]{2,1,0:T(8,128)S(1)} %select_maximum_fusion.12, f32[12,128,256]{2,1,0:T(8,128)S(1)} %get-tuple-element.79, ...), kind=kLoop, calls=%fused_computation.171 | loop fusion | flops 10747904 | bytes 23199744 | tf_op jit(solution)/shard_map/add | solution.py:167
  44.0 1.5 scatter-add.14
  45.5 1.1 fusion.180
  46.6 2.3 %collective-permute-start.4 = (f32[4,128,256]{2,1,0:T(8,128)}, f32[4,128,256]{2,1,0:T(8,128)S(1)}, u32[]{:S(2)}, u32[]{:S(2)}) collective-permute-start(f32[4,128,256]{2,1,0:T(8,128)} %get-tuple-element.75), channel_id=1, source_target_pairs={{4,0},{8,4},{12,8},{16,12},{20,16},{24,20},{28,24},{32,28},{36,32}... | collective-permute-start | bytes 1572872 | tf_op jit(solution)/shard_map/ppermute | solution.py:37
  48.9 3.3 %collective-permute-start.5 = (f32[4,128,256]{2,1,0:T(8,128)}, f32[4,128,256]{2,1,0:T(8,128)S(1)}, u32[]{:S(2)}, u32[]{:S(2)}) collective-permute-start(f32[4,128,256]{2,1,0:T(8,128)} %get-tuple-element.76), channel_id=1, source_target_pairs={{0,4},{4,8},{8,12},{12,16},{16,20},{20,24},{24,28},{28,32},{32,36}... | collective-permute-start | bytes 1572872 | tf_op jit(solution)/shard_map/ppermute | solution.py:36
  52.1 1.3 collective-permute-start.6
  53.4 4.2 %collective-permute-start.7 = (f32[8,4,256]{2,1,0:T(4,128)S(1)}, f32[8,4,256]{2,1,0:T(4,128)S(1)}, u32[]{:S(2)}, u32[]{:S(2)}) collective-permute-start(f32[8,4,256]{2,1,0:T(4,128)S(1)} %get-tuple-element.73), channel_id=1, source_target_pairs={{0,1},{1,2},{2,3},{4,5},{5,6},{6,7},{8,9},{9,10},{10,11},{12,13},{... | collective-permute-start | bytes 98312 | tf_op jit(solution)/shard_map/ppermute | solution.py:36
  57.6 1.0 copy.82
  59.7 3.3 %select_maximum_fusion.8 = f32[16,136,264]{2,1,0:T(8,128)S(1)} fusion(f32[16,4,256]{2,1,0:T(4,128)S(1)} %pad.49, f32[16,4,256]{2,1,0:T(4,128)S(1)} %pad.50, f32[4,128,256]{2,1,0:T(8,128)S(1)} %collective-permute-done.4, f32[8,128,256]{2,1,0:T(8,128)S(1)} %scatter-add.14, f32[4,128,256]{2,1,0:T(8,128)S(1)} %collective-permute-done.5), kind=kLoop, calls=%fused_computation.16 | loop fusion | flops 6893568 | bytes 4526080 | tf_op jit(solution)/shard_map/concatenate | solution.py:43
  63.0 4.0 %fusion.72 = f32[8,128,256]{2,1,0:T(8,128)S(1)} fusion(f32[8,128,256]{2,1,0:T(8,128)S(1)} %copy-done, f32[8,128,256]{2,1,0:T(8,128)S(1)} %scatter-add.14, f32[4,128,256]{2,1,0:T(8,128)} %copy-done.9, f32[4,128,256]{2,1,0:T(8,128)} %copy-done.7, f32[16,136,264]{2,1,0:T(8,128)S(1)} %select_maximum_fusion.8, f32[16,132,256]{2,1,0:T(8,128)S(1)} %get-tuple-element.64, ...), kind=kLoop, calls=%fused_computation.143 | loop fusion | flops 10747904 | bytes 22020096 | tf_op jit(solution)/shard_map/add | solution.py:167
  67.2 1.5 scatter-add.15
  68.8 1.1 fusion.178
  69.8 2.1 collective-permute-start.8
  71.9 3.8 %collective-permute-start.9 = (f32[4,128,256]{2,1,0:T(8,128)}, f32[4,128,256]{2,1,0:T(8,128)S(1)}, u32[]{:S(2)}, u32[]{:S(2)}) collective-permute-start(f32[4,128,256]{2,1,0:T(8,128)} %get-tuple-element.72), channel_id=1, source_target_pairs={{0,4},{4,8},{8,12},{12,16},{16,20},{20,24},{24,28},{28,32},{32,36}... | collective-permute-start | bytes 1572872 | tf_op jit(solution)/shard_map/ppermute | solution.py:36
  75.7 1.3 collective-permute-start.10
  77.0 4.2 %collective-permute-start.11 = (f32[8,4,256]{2,1,0:T(4,128)S(1)}, f32[8,4,256]{2,1,0:T(4,128)S(1)}, u32[]{:S(2)}, u32[]{:S(2)}) collective-permute-start(f32[8,4,256]{2,1,0:T(4,128)S(1)} %get-tuple-element.69), channel_id=1, source_target_pairs={{0,1},{1,2},{2,3},{4,5},{5,6},{6,7},{8,9},{9,10},{10,11},{12,13},{... | collective-permute-start | bytes 98312 | tf_op jit(solution)/shard_map/ppermute | solution.py:36
  81.3 1.0 copy.83
  83.3 3.3 %select_maximum_fusion.4 = f32[16,136,264]{2,1,0:T(8,128)S(1)} fusion(f32[16,4,256]{2,1,0:T(4,128)S(1)} %pad.52, f32[16,4,256]{2,1,0:T(4,128)S(1)} %pad.53, f32[4,128,256]{2,1,0:T(8,128)S(1)} %collective-permute-done.8, f32[8,128,256]{2,1,0:T(8,128)S(1)} %scatter-add.15, f32[4,128,256]{2,1,0:T(8,128)S(1)} %collective-permute-done.9), kind=kLoop, calls=%fused_computation.12 | loop fusion | flops 6893568 | bytes 4526080 | tf_op jit(solution)/shard_map/concatenate | solution.py:43
  86.7 4.0 %fusion.42 = f32[8,128,256]{2,1,0:T(8,128)S(1)} fusion(f32[8,128,256]{2,1,0:T(8,128)S(1)} %copy-done.1, f32[8,128,256]{2,1,0:T(8,128)S(1)} %scatter-add.15, f32[4,128,256]{2,1,0:T(8,128)} %copy-done.10, f32[4,128,256]{2,1,0:T(8,128)} %copy-done.8, f32[16,136,264]{2,1,0:T(8,128)S(1)} %select_maximum_fusion.4, f32[16,132,256]{2,1,0:T(8,128)S(1)} %get-tuple-element.62, ...), kind=kLoop, calls=%fused_computation.113 | loop fusion | flops 10747904 | bytes 22020096 | tf_op jit(solution)/shard_map/add | solution.py:167
  90.7 1.0 slice_add_fusion.19
  91.7 2.2 %scatter-add.16 = f32[8,128,256]{2,1,0:T(8,128)S(1)} dynamic-update-slice(f32[8,128,256]{2,1,0:T(8,128)S(1)} %fusion.42, f32[8,128,1]{2,1,0:T(8,128)} %slice_add_fusion.19, s32[]{:T(128)} %constant.136.clone.1, s32[]{:T(128)} %constant.136.clone.1, s32[]{:T(128)} %constant.138.clone.1) | dynamic-update-slice | bytes 8196 | tf_op jit(solution)/shard_map/scatter-add | solution.py:168
  93.9 1.1 fusion.176
  95.0 1.9 collective-permute-start.12
  96.9 3.9 %collective-permute-start.13 = (f32[4,128,256]{2,1,0:T(8,128)}, f32[4,128,256]{2,1,0:T(8,128)}, u32[]{:S(2)}, u32[]{:S(2)}) collective-permute-start(f32[4,128,256]{2,1,0:T(8,128)} %get-tuple-element.68), channel_id=1, source_target_pairs={{0,4},{4,8},{8,12},{12,16},{16,20},{20,24},{24,28},{28,32},{32,36}... | collective-permute-start | bytes 1572872 | tf_op jit(solution)/shard_map/ppermute | solution.py:36
  100.8 1.3 collective-permute-start.14
  102.1 4.5 %collective-permute-start.15 = (f32[8,4,256]{2,1,0:T(4,128)S(1)}, f32[8,4,256]{2,1,0:T(4,128)S(1)}, u32[]{:S(2)}, u32[]{:S(2)}) collective-permute-start(f32[8,4,256]{2,1,0:T(4,128)S(1)} %get-tuple-element.65), channel_id=1, source_target_pairs={{0,1},{1,2},{2,3},{4,5},{5,6},{6,7},{8,9},{9,10},{10,11},{12,13},{... | collective-permute-start | bytes 98312 | tf_op jit(solution)/shard_map/ppermute | solution.py:36
  106.6 1.0 copy.84
  107.7 1.9 pad_maximum_fusion.2
  109.6 2.4 %select_maximum_fusion = f32[16,136,264]{2,1,0:T(8,128)S(1)} fusion(f32[16,4,256]{2,1,0:T(4,128)S(1)} %pad.55, f32[16,4,256]{2,1,0:T(4,128)S(1)} %pad.56, f32[4,128,256]{2,1,0:T(8,128)} %collective-permute-done.12, f32[8,128,256]{2,1,0:T(8,128)S(1)} %scatter-add.16, f32[4,128,256]{2,1,0:T(8,128)} %collective-permute-done.13), kind=kLoop, calls=%fused_computation.8 | loop fusion | flops 6893568 | bytes 4526080 | tf_op jit(solution)/shard_map/concatenate | solution.py:43
  112.0 3.9 %fusion.12 = f32[8,128,256]{2,1,0:T(8,128)S(1)} fusion(f32[8,128,256]{2,1,0:T(8,128)S(1)} %copy-done.2, f32[8,128,256]{2,1,0:T(8,128)S(1)} %scatter-add.16, f32[4,128,256]{2,1,0:T(8,128)} %collective-permute-done.13, f32[4,128,256]{2,1,0:T(8,128)} %collective-permute-done.12, f32[16,136,264]{2,1,0:T(8,128)S(1)} %select_maximum_fusion, ...), kind=kLoop, calls=%fused_computation.83 | loop fusion | flops 10747904 | bytes 22020096 | tf_op jit(solution)/shard_map/add | solution.py:167
  117.9 2.7 %scatter-add.19 = f32[8,128,256]{2,1,0:T(8,128)} dynamic-update-slice(f32[8,128,256]{2,1,0:T(8,128)} %copy-done.6, f32[8,128,1]{2,1,0:T(8,128)} %slice_add_fusion.18, s32[]{:T(128)} %constant.136.clone.1, s32[]{:T(128)} %constant.136.clone.1, s32[]{:T(128)} %constant.138.clone.1) | dynamic-update-slice | bytes 8196 | tf_op jit(solution)/shard_map/scatter-add | solution.py:168
  120.6 2.4 %fusion.129 = f32[8,128,256]{2,1,0:T(8,128)S(1)} fusion(f32[8,128,256]{2,1,0:T(8,128)} %scatter-add.19, f32[8,128,256]{2,1,0:T(8,128)S(1)} %scatter-add.16, f32[8,128,256]{2,1,0:T(8,128)S(1)} %scatter-add.15, f32[8,128,256]{2,1,0:T(8,128)S(1)} %scatter-add.14, bf16[4,8,128,256]{3,2,1,0:T(8,128)(2,1)} %param.24), kind=kLoop, calls=%fused_computation.227 | loop fusion | flops 3145728 | bytes 7340032 | tf_op jit(solution)/shard_map/mul | solution.py:171
  123.0 1.6 copy.85
  124.6 16.0 %all-to-all-start.1 = ((f32[8,128,256]{2,0,1:T(8,128)}), f32[8,128,256]{2,0,1:T(8,128)S(1)}, u32[]{:S(2)}, u32[]{:S(2)}) async-start(f32[8,128,256]{2,0,1:T(8,128)} %copy.85), calls=%async_computation.1 | async-start | bytes 2097152 | tf_op jit(solution)/shard_map/all_to_all | solution.py:174
  140.6 28.2 %all-to-all-done.1 = f32[8,128,256]{2,0,1:T(8,128)S(1)} async-done(((f32[8,128,256]{2,0,1:T(8,128)}), f32[8,128,256]{2,0,1:T(8,128)S(1)}, u32[]{:S(2)}, u32[]{:S(2)}) %all-to-all-start.1) | async-done | bytes 1048608 | tf_op jit(solution)/shard_map/all_to_all | solution.py:174
  169.7 2.5 %fusion.132 = f32[512,2,256]{2,0,1:T(8,128)S(1)} fusion(f32[2,256,512]{2,1,0:T(8,128)S(1)} %bitcast.48, f32[512]{0:T(512)S(1)} %iota_convert_fusion), kind=kOutput, calls=%fused_computation.233 | convolution fusion | flops 1614282752 | bytes 2099200 | tf_op jit(solution)/shard_map/dot_general | solution.py:175
  173.1 34.2 %all_to_all.38 = f32[512,2,256]{2,1,0:T(2,128)S(1)} all-to-all(f32[512,2,256]{2,1,0:T(2,128)S(1)} %copy.88), channel_id=1, replica_groups=mesh['gx'=64,'gy'=4] {'gx'}, dimensions={0} | all-to-all | bytes 2097152 | tf_op jit(solution)/shard_map/all_to_all | solution.py:181
  208.5 3.6 %divide_subtract_fusion = (f32[8,128,256]{2,1,0:T(8,128)}, f32[8,128,256]{2,1,0:T(8,128)}, f32[8,128,256]{2,1,0:T(8,128)}) fusion(f32[8,128,256]{2,1,0:T(8,128)S(1)} %copy-done.3, f32[8,128,256]{2,1,0:T(8,128)S(1)} %all_to_all.34, f32[8,128,256]{2,1,0:T(8,128)} %param.20, f32[8,128,256]{2,1,0:T(8,128)} %param.21), kind=kLoop, calls=%fused_computation.236 | loop fusion | flops 3145728 | bytes 7340032 | tf_op jit(solution)/shard_map/sub | solution.py:184
  (105 shorter events, 11.7 us)
Async XLA Ops:
  0.6 23.7 %copy-start.4 = (f32[8,128,256]{2,1,0:T(8,128)S(1)}, f32[8,128,256]{2,1,0:T(8,128)}, u32[]{:S(2)}) copy-start(f32[8,128,256]{2,1,0:T(8,128)} %param.23) | copy-start | bytes 3145732
  0.6 8.9 %copy-start.17 = (s32[1,128,1]{1,2,0:T(1,128)S(1)}, s32[1,128,1]{1,2,0:T(1,128)}, u32[]{:S(2)}) copy-start(s32[1,128,1]{1,2,0:T(1,128)} %param.26) | copy-start | bytes 1540
  0.7 9.1 %copy-start.16 = (f32[1,128,128]{2,1,0:T(8,128)S(1)}, f32[1,128,128]{2,1,0:T(8,128)}, u32[]{:S(2)}) copy-start(f32[1,128,128]{2,1,0:T(8,128)} %param.25) | copy-start | bytes 196612
  0.7 9.2 %copy-start.19 = (s32[16]{0:T(128)S(1)}, s32[16]{0:T(128)}, u32[]{:S(2)}) copy-start(s32[16]{0:T(128)} %param.29) | copy-start | bytes 196
  0.7 9.2 %copy-start.20 = (s32[1,128]{1,0:T(1,128)S(1)}, s32[1,128]{1,0:T(1,128)}, u32[]{:S(2)}) copy-start(s32[1,128]{1,0:T(1,128)} %param.28) | copy-start | bytes 1540
  0.7 9.3 %copy-start.18 = (s32[1,128]{1,0:T(1,128)S(1)}, s32[1,128]{1,0:T(1,128)}, u32[]{:S(2)}) copy-start(s32[1,128]{1,0:T(1,128)} %param.27) | copy-start | bytes 1540
  2.1 36.3 %collective-permute-start.1 = (f32[4,128,256]{2,1,0:T(8,128)S(1)}, f32[4,128,256]{2,1,0:T(8,128)S(1)}, u32[]{:S(2)}, u32[]{:S(2)}) collective-permute-start(f32[4,128,256]{2,1,0:T(8,128)S(1)} %get-tuple-element.83), channel_id=1, source_target_pairs={{0,4},{4,8},{8,12},{12,16},{16,20},{20,24},{24,28},{28,32},{32,36}... | collective-permute-start | bytes 1572872 | tf_op jit(solution)/shard_map/ppermute | solution.py:36
  6.7 32.2 %collective-permute-start = (f32[4,128,256]{2,1,0:T(8,128)S(1)}, f32[4,128,256]{2,1,0:T(8,128)S(1)}, u32[]{:S(2)}, u32[]{:S(2)}) collective-permute-start(f32[4,128,256]{2,1,0:T(8,128)S(1)} %get-tuple-element.82), channel_id=1, source_target_pairs={{4,0},{8,4},{12,8},{16,12},{20,16},{24,20},{28,24},{32,28},{36,32}... | collective-permute-start | bytes 1572872 | tf_op jit(solution)/shard_map/ppermute | solution.py:37
  11.4 24.0 %all-to-all-start = ((f32[64,4,5]{2,1,0:T(4,128)}), f32[64,4,5]{2,1,0:T(4,128)S(1)}, u32[]{:S(2)}, u32[]{:S(2)}) async-start(f32[64,4,5]{2,1,0:T(4,128)} %copy.79), calls=%async_computation | async-start | bytes 262144 | tf_op jit(solution)/shard_map/all_to_all | solution.py:53
  24.4 14.0 %collective-permute-start.2 = (f32[8,4,256]{2,1,0:T(4,128)S(1)}, f32[8,4,256]{2,1,0:T(4,128)S(1)}, u32[]{:S(2)}, u32[]{:S(2)}) collective-permute-start(f32[8,4,256]{2,1,0:T(4,128)S(1)} %get-tuple-element.80), channel_id=1, source_target_pairs={{1,0},{2,1},{3,2},{5,4},{6,5},{7,6},{9,8},{10,9},{11,10},{13,12},{... | collective-permute-start | bytes 98312 | tf_op jit(solution)/shard_map/ppermute | solution.py:37
  25.7 12.7 %collective-permute-start.3 = (f32[8,4,256]{2,1,0:T(4,128)S(1)}, f32[8,4,256]{2,1,0:T(4,128)S(1)}, u32[]{:S(2)}, u32[]{:S(2)}) collective-permute-start(f32[8,4,256]{2,1,0:T(4,128)S(1)} %get-tuple-element.81), channel_id=1, source_target_pairs={{0,1},{1,2},{2,3},{4,5},{5,6},{6,7},{8,9},{9,10},{10,11},{12,13},{... | collective-permute-start | bytes 98312 | tf_op jit(solution)/shard_map/ppermute | solution.py:36
  38.9 1.2 copy-start
  38.9 1.5 copy-start.15
  40.5 3.3 %copy-start.11 = (f32[8,128,1]{2,1,0:T(8,128)S(1)}, f32[8,128,1]{2,1,0:T(8,128)}, u32[]{:S(2)}) copy-start(f32[8,128,1]{2,1,0:T(8,128)} %copy.81) | copy-start | bytes 12292
  46.6 12.1 %collective-permute-start.4 = (f32[4,128,256]{2,1,0:T(8,128)}, f32[4,128,256]{2,1,0:T(8,128)S(1)}, u32[]{:S(2)}, u32[]{:S(2)}) collective-permute-start(f32[4,128,256]{2,1,0:T(8,128)} %get-tuple-element.75), channel_id=1, source_target_pairs={{4,0},{8,4},{12,8},{16,12},{20,16},{24,20},{28,24},{32,28},{36,32}... | collective-permute-start | bytes 1572872 | tf_op jit(solution)/shard_map/ppermute | solution.py:37
  48.9 9.9 %collective-permute-start.5 = (f32[4,128,256]{2,1,0:T(8,128)}, f32[4,128,256]{2,1,0:T(8,128)S(1)}, u32[]{:S(2)}, u32[]{:S(2)}) collective-permute-start(f32[4,128,256]{2,1,0:T(8,128)} %get-tuple-element.76), channel_id=1, source_target_pairs={{0,4},{4,8},{8,12},{12,16},{16,20},{20,24},{24,28},{28,32},{32,36}... | collective-permute-start | bytes 1572872 | tf_op jit(solution)/shard_map/ppermute | solution.py:36
  52.1 6.5 %collective-permute-start.6 = (f32[8,4,256]{2,1,0:T(4,128)S(1)}, f32[8,4,256]{2,1,0:T(4,128)S(1)}, u32[]{:S(2)}, u32[]{:S(2)}) collective-permute-start(f32[8,4,256]{2,1,0:T(4,128)S(1)} %get-tuple-element.74), channel_id=1, source_target_pairs={{1,0},{2,1},{3,2},{5,4},{6,5},{7,6},{9,8},{10,9},{11,10},{13,12},{... | collective-permute-start | bytes 98312 | tf_op jit(solution)/shard_map/ppermute | solution.py:37
  53.4 5.2 %collective-permute-start.7 = (f32[8,4,256]{2,1,0:T(4,128)S(1)}, f32[8,4,256]{2,1,0:T(4,128)S(1)}, u32[]{:S(2)}, u32[]{:S(2)}) collective-permute-start(f32[8,4,256]{2,1,0:T(4,128)S(1)} %get-tuple-element.73), channel_id=1, source_target_pairs={{0,1},{1,2},{2,3},{4,5},{5,6},{6,7},{8,9},{9,10},{10,11},{12,13},{... | collective-permute-start | bytes 98312 | tf_op jit(solution)/shard_map/ppermute | solution.py:36
  58.7 0.8 copy-start.7
  58.7 0.9 copy-start.9
  59.7 3.3 %copy-start.5 = (f32[8,128,256]{2,1,0:T(8,128)S(1)}, f32[8,128,256]{2,1,0:T(8,128)}, u32[]{:S(2)}) copy-start(f32[8,128,256]{2,1,0:T(8,128)} %param.23) | copy-start | bytes 3145732
  63.0 4.0 %copy-start.13 = (f32[8,128,1]{2,1,0:T(8,128)S(1)}, f32[8,128,1]{2,1,0:T(8,128)}, u32[]{:S(2)}) copy-start(f32[8,128,1]{2,1,0:T(8,128)} %copy.82) | copy-start | bytes 12292
  69.8 12.5 %collective-permute-start.8 = (f32[4,128,256]{2,1,0:T(8,128)}, f32[4,128,256]{2,1,0:T(8,128)S(1)}, u32[]{:S(2)}, u32[]{:S(2)}) collective-permute-start(f32[4,128,256]{2,1,0:T(8,128)} %get-tuple-element.71), channel_id=1, source_target_pairs={{4,0},{8,4},{12,8},{16,12},{20,16},{24,20},{28,24},{32,28},{36,32}... | collective-permute-start | bytes 1572872 | tf_op jit(solution)/shard_map/ppermute | solution.py:37
  71.9 10.4 %collective-permute-start.9 = (f32[4,128,256]{2,1,0:T(8,128)}, f32[4,128,256]{2,1,0:T(8,128)S(1)}, u32[]{:S(2)}, u32[]{:S(2)}) collective-permute-start(f32[4,128,256]{2,1,0:T(8,128)} %get-tuple-element.72), channel_id=1, source_target_pairs={{0,4},{4,8},{8,12},{12,16},{16,20},{20,24},{24,28},{28,32},{32,36}... | collective-permute-start | bytes 1572872 | tf_op jit(solution)/shard_map/ppermute | solution.py:36
  75.7 6.6 %collective-permute-start.10 = (f32[8,4,256]{2,1,0:T(4,128)S(1)}, f32[8,4,256]{2,1,0:T(4,128)S(1)}, u32[]{:S(2)}, u32[]{:S(2)}) collective-permute-start(f32[8,4,256]{2,1,0:T(4,128)S(1)} %get-tuple-element.70), channel_id=1, source_target_pairs={{1,0},{2,1},{3,2},{5,4},{6,5},{7,6},{9,8},{10,9},{11,10},{13,12},{... | collective-permute-start | bytes 98312 | tf_op jit(solution)/shard_map/ppermute | solution.py:37
  77.0 5.3 %collective-permute-start.11 = (f32[8,4,256]{2,1,0:T(4,128)S(1)}, f32[8,4,256]{2,1,0:T(4,128)S(1)}, u32[]{:S(2)}, u32[]{:S(2)}) collective-permute-start(f32[8,4,256]{2,1,0:T(4,128)S(1)} %get-tuple-element.69), channel_id=1, source_target_pairs={{0,1},{1,2},{2,3},{4,5},{5,6},{6,7},{8,9},{9,10},{10,11},{12,13},{... | collective-permute-start | bytes 98312 | tf_op jit(solution)/shard_map/ppermute | solution.py:36
  82.4 0.8 copy-start.8
  82.4 0.9 copy-start.10
  83.3 3.3 %copy-start.1 = (f32[8,128,256]{2,1,0:T(8,128)S(1)}, f32[8,128,256]{2,1,0:T(8,128)}, u32[]{:S(2)}) copy-start(f32[8,128,256]{2,1,0:T(8,128)} %param.19) | copy-start | bytes 3145732
  86.7 4.0 %copy-start.14 = (f32[8,128,1]{2,1,0:T(8,128)S(1)}, f32[8,128,1]{2,1,0:T(8,128)}, u32[]{:S(2)}) copy-start(f32[8,128,1]{2,1,0:T(8,128)} %copy.83) | copy-start | bytes 12292
  95.0 12.7 %collective-permute-start.12 = (f32[4,128,256]{2,1,0:T(8,128)}, f32[4,128,256]{2,1,0:T(8,128)}, u32[]{:S(2)}, u32[]{:S(2)}) collective-permute-start(f32[4,128,256]{2,1,0:T(8,128)} %get-tuple-element.67), channel_id=1, source_target_pairs={{4,0},{8,4},{12,8},{16,12},{20,16},{24,20},{28,24},{32,28},{36,32}... | collective-permute-start | bytes 1572872 | tf_op jit(solution)/shard_map/ppermute | solution.py:37
  96.9 10.8 %collective-permute-start.13 = (f32[4,128,256]{2,1,0:T(8,128)}, f32[4,128,256]{2,1,0:T(8,128)}, u32[]{:S(2)}, u32[]{:S(2)}) collective-permute-start(f32[4,128,256]{2,1,0:T(8,128)} %get-tuple-element.68), channel_id=1, source_target_pairs={{0,4},{4,8},{8,12},{12,16},{16,20},{20,24},{24,28},{28,32},{32,36}... | collective-permute-start | bytes 1572872 | tf_op jit(solution)/shard_map/ppermute | solution.py:36
  100.8 6.8 %collective-permute-start.14 = (f32[8,4,256]{2,1,0:T(4,128)S(1)}, f32[8,4,256]{2,1,0:T(4,128)S(1)}, u32[]{:S(2)}, u32[]{:S(2)}) collective-permute-start(f32[8,4,256]{2,1,0:T(4,128)S(1)} %get-tuple-element.66), channel_id=1, source_target_pairs={{1,0},{2,1},{3,2},{5,4},{6,5},{7,6},{9,8},{10,9},{11,10},{13,12},{... | collective-permute-start | bytes 98312 | tf_op jit(solution)/shard_map/ppermute | solution.py:37
  102.1 5.5 %collective-permute-start.15 = (f32[8,4,256]{2,1,0:T(4,128)S(1)}, f32[8,4,256]{2,1,0:T(4,128)S(1)}, u32[]{:S(2)}, u32[]{:S(2)}) collective-permute-start(f32[8,4,256]{2,1,0:T(4,128)S(1)} %get-tuple-element.65), channel_id=1, source_target_pairs={{0,1},{1,2},{2,3},{4,5},{5,6},{6,7},{8,9},{9,10},{10,11},{12,13},{... | collective-permute-start | bytes 98312 | tf_op jit(solution)/shard_map/ppermute | solution.py:36
  109.6 2.4 %copy-start.2 = (f32[8,128,256]{2,1,0:T(8,128)S(1)}, f32[8,128,256]{2,1,0:T(8,128)}, u32[]{:S(2)}) copy-start(f32[8,128,256]{2,1,0:T(8,128)} %param.19) | copy-start | bytes 3145732
  112.0 4.9 %copy-start.12 = (f32[8,128,1]{2,1,0:T(8,128)S(1)}, f32[8,128,1]{2,1,0:T(8,128)}, u32[]{:S(2)}) copy-start(f32[8,128,1]{2,1,0:T(8,128)} %copy.84) | copy-start | bytes 12292
  116.0 1.0 copy-start.6
  124.6 44.2 %all-to-all-start.1 = ((f32[8,128,256]{2,0,1:T(8,128)}), f32[8,128,256]{2,0,1:T(8,128)S(1)}, u32[]{:S(2)}, u32[]{:S(2)}) async-start(f32[8,128,256]{2,0,1:T(8,128)} %copy.85), calls=%async_computation.1 | async-start | bytes 2097152 | tf_op jit(solution)/shard_map/all_to_all | solution.py:174
  207.3 1.2 copy-start.3
where the time goes:
time: 213 us; the launch traced here: 212 us
  starting transfers between devices  74.6 us (35%)
  other arithmetic  38.9 us (18%)
  blocking collectives  34.2 us (16%)
  waiting for transfers between devices  34 us (16%)
  local copies, waits for them, and re-layouts  25.6 us (12%)
  matrix products  3.33 us (2%)
    all_to_all x1, blocking collectives, shards(): lax.all_to_all(result, 'gx', split_axis=0, concat_axis=1, tiled=True)  34.2 us
    ppermute x8, starting transfers between devices, padded_2(): lax.ppermute(last, axis, up)  32.3 us
    all_to_all x1, waiting for transfers between devices, shards(): lax.all_to_all(gradient, 'gx', split_axis=1, concat_axis=0, tiled=True)  28.2 us
    all_to_all x1, starting transfers between devices, shards(): lax.all_to_all(gradient, 'gx', split_axis=1, concat_axis=0, tiled=True)  16 us
    add x4, other arithmetic, shards(): following = 2.0 * current - previous + courant * laplacian(current)  15.1 us
    ppermute x8, starting transfers between devices, padded_2(): lax.ppermute(first, axis, [(b, a) for a, b in up])  13.4 us
    all_to_all x1, starting transfers between devices, sent_together(): lax.all_to_all(both, axis, split_axis=split_dim, concat_axis=concat_dim,...  12.9 us
    concatenate x7, other arithmetic, padded_2(): jnp.concatenate([jnp.pad(low, around), array, jnp.pad(high, around)], axi...  12.8 us
  transfers between devices with their start and end apart: 18, of which 2 were waited for; matrix products, arithmetic and copies ran while one was open for 4% of the time, Pallas kernels for 0%

commit v1 on v0

v1 whole, which is shorter than its diff:
```python
import math

import jax
import jax.numpy as jnp
import numpy as np
from jax import lax
from jax.experimental import pallas as pl
from jax.experimental.pallas import tpu as pltpu
from jax.sharding import PartitionSpec as P

MESH = pl.DeviceIdType.MESH
F32 = jnp.float32
HIGHEST = lax.Precision.HIGHEST

STEPS = 4
SAMPLES_PER_STEP = 32
ZREC = 8
SHOTS = 16
NG = 64
NYD = 4
NQ = 8
NZD = 8
CX, CY, NZ = 8, 128, 256
BLOCKS = 128
SLOTS = 4
ROWS = 32
CHUNKS = CY // ROWS
SEG = CY // NQ

coefficients = (8.0 / 5.0, -1.0 / 5.0, 8.0 / 315.0, -1.0 / 560.0)
center_weight = -205.0 / 72.0
smooth_length = 4096.0
cosh_value = 1.0 + 0.5 / smooth_length
theta = math.log(cosh_value + math.sqrt(cosh_value * cosh_value - 1.0))
image_gain = 10.0
beta_first = 0.9
beta_second = 0.999
bias_first = 1.0 - 0.9**10
bias_second = 1.0 - 0.999**10
learning_rate = 0.01
epsilon = 1e-08


def depth_table():
    table = np.zeros((NZ, NZ), np.float64)
    for i in range(NZ):
        table[i, i] = 3.0 * center_weight
        for k, w in enumerate(coefficients, 1):
            if i + k < NZ:
                table[i + k, i] = w
                table[i, i + k] = w
    return table.astype(np.float32)


def smoother_factors(count):
    position = np.arange(count, dtype=np.float64)
    scale = math.sqrt(image_gain / (smooth_length * math.sinh(theta) * math.sinh(theta * (count + 1))))
    rise = scale * np.sinh(theta * (position + 1.0))
    fall = scale * np.sinh(theta * (count - position))
    return np.concatenate([rise, fall]).astype(np.float32)


def iota(shape, dim):
    return lax.broadcasted_iota(jnp.int32, shape, dim)


def window_kernel(
    rollback_ref,
    factor_ref,
    table_ref,
    traces_ref,
    slab_ref,
    cell_ref,
    shot_ref,
    courant_hbm,
    prev_hbm,
    now_hbm,
    forward_hbm,
    image_hbm,
    last_hbm,
    sums_hbm,
    field,
    courant,
    forward,
    image,
    source,
    packed,
    landed,
    depth,
    plane,
    group_in,
    total,
    line_in,
    back,
    sums,
    load_sem,
    trace_send,
    trace_recv,
    x_send,
    x_recv,
    y_send,
    y_recv,
    group_send,
    group_recv,
    line_send,
    line_recv,
    back_send,
    back_recv,
    store_sem,
):
    gx = lax.axis_index("gx")
    gy = lax.axis_index("gy")
    own_z = gx // NQ
    own_q = gx % NQ

    loads = [
        pltpu.make_async_copy(
            now_hbm, field.at[0, pl.ds(4, CX), pl.ds(8, CY), :], load_sem.at[0]
        ),
        pltpu.make_async_copy(
            prev_hbm, field.at[1, pl.ds(4, CX), pl.ds(8, CY), :], load_sem.at[1]
        ),
        pltpu.make_async_copy(courant_hbm, courant, load_sem.at[2]),
        pltpu.make_async_copy(forward_hbm, forward, load_sem.at[3]),
    ]
    for copy in loads:
        copy.start()

    @pl.when(gx == 0)
    def _():
        field[:, 0:4, 8 : 8 + CY, :] = jnp.zeros((2, 4, CY, NZ), F32)

    @pl.when(gx == NG - 1)
    def _():
        field[:, 12:16, 8 : 8 + CY, :] = jnp.zeros((2, 4, CY, NZ), F32)

    @pl.when(gy == 0)
    def _():
        field[:, 4:12, 0:8, :] = jnp.zeros((2, CX, 8, NZ), F32)

    @pl.when(gy == NYD - 1)
    def _():
        field[:, 4:12, 8 + CY : 16 + CY, :] = jnp.zeros((2, CX, 8, NZ), F32)

    barrier = pltpu.get_barrier_semaphore()

    def greet(k, carry):
        pl.semaphore_signal(
            barrier, inc=1, device_id={"gx": (gx + k) % NG}, device_id_type=MESH
        )
        return carry

    lax.fori_loop(1, NG, greet, 0)
    for k in (1, NYD - 1):
        pl.semaphore_signal(
            barrier, inc=1, device_id={"gy": (gy + k) % NYD}, device_id_type=MESH
        )

    rows = iota((BLOCKS, 128), 0)
    lanes = iota((BLOCKS, 128), 1)
    diagonal = rows == lanes
    slab_col = slab_ref[0]
    shot_row = shot_ref[...]
    cell_row = cell_ref[...].astype(F32)
    live_row = jnp.zeros((1, 128), F32)
    for s in range(SHOTS):
        flag = jnp.where(rollback_ref[s] == 0, 1.0, 0.0)
        live_row = jnp.where(shot_row == s, flag, live_row)
    live_col = jnp.sum(jnp.where(diagonal, live_row, 0.0), axis=1, keepdims=True)
    cell_col = jnp.sum(jnp.where(diagonal, cell_row, 0.0), axis=1, keepdims=True)
    slab_float = slab_col.astype(F32)
    slab_row = jnp.sum(jnp.where(diagonal, slab_float, 0.0), axis=0, keepdims=True)
    slot_col = jnp.sum(
        jnp.where((slab_float == slab_row) & (lanes < rows), 1.0, 0.0), axis=1, keepdims=True
    )
    pick = jnp.where((lanes % 8 == rows // SAMPLES_PER_STEP) & (lanes < 8 * SLOTS), 1.0, 0.0)
    reduced = jnp.dot(traces_ref[0], pick, precision=HIGHEST, preferred_element_type=F32)
    entries = reduced * live_col + jnp.where(lanes % 8 == STEPS, cell_col, 0.0)
    entries = jnp.where(slot_col == (lanes // 8).astype(F32), entries, 0.0)
    named = jnp.where(iota((NG, BLOCKS), 0).astype(F32) == slab_row, 1.0, 0.0)
    packed[...] = jnp.dot(
        named, entries, precision=HIGHEST, preferred_element_type=F32
    ).reshape(NG, 1, 128)

    pl.semaphore_wait(barrier, NG - 1 + 2)

    def x_copies(parity, chunk, source_low, source_high):
        band = pl.ds(pl.multiple_of(8 + chunk * ROWS, 8), ROWS)
        low = pltpu.make_async_remote_copy(
            src_ref=source_low,
            dst_ref=field.at[parity, pl.ds(12, 4), band, :],
            send_sem=x_send.at[parity, 0, chunk],
            recv_sem=x_recv.at[parity, 1, chunk],
            device_id={"gx": (gx + NG - 1) % NG},
            device_id_type=MESH,
        )
        high = pltpu.make_async_remote_copy(
            src_ref=source_high,
            dst_ref=field.at[parity, pl.ds(0, 4), band, :],
            send_sem=x_send.at[parity, 1, chunk],
            recv_sem=x_recv.at[parity, 0, chunk],
            device_id={"gx": (gx + 1) % NG},
            device_id_type=MESH,
        )
        return low, high

    def x_field(parity, chunk):
        band = pl.ds(pl.multiple_of(8 + chunk * ROWS, 8), ROWS)
        return x_copies(
            parity, chunk, field.at[parity, pl.ds(4, 4), band, :], field.at[parity, pl.ds(8, 4), band, :]
        )

    def y_copies(parity, source_low, source_high):
        low = pltpu.make_async_remote_copy(
            src_ref=source_low,
            dst_ref=field.at[parity, pl.ds(4, CX), pl.ds(8 + CY, 8), :],
            send_sem=y_send.at[parity, 0],
            recv_sem=y_recv.at[parity, 1],
            device_id={"gy": (gy + NYD - 1) % NYD},
            device_id_type=MESH,
        )
        high = pltpu.make_async_remote_copy(
            src_ref=source_high,
            dst_ref=field.at[parity, pl.ds(4, CX), pl.ds(0, 8), :],
            send_sem=y_send.at[parity, 1],
            recv_sem=y_recv.at[parity, 0],
            device_id={"gy": (gy + 1) % NYD},
            device_id_type=MESH,
        )
        return low, high

    def y_field(parity):
        return y_copies(
            parity,
            field.at[parity, pl.ds(4, CX), pl.ds(8, 8), :],
            field.at[parity, pl.ds(4, CX), pl.ds(CY, 8), :],
        )

    has_low, has_high = gx > 0, gx < NG - 1
    y_has_low, y_has_high = gy > 0, gy < NYD - 1

    def order(i):
        return (CHUNKS - i) % CHUNKS

    now_low, now_high = y_copies(0, now_hbm.at[:, pl.ds(0, 8), :], now_hbm.at[:, pl.ds(CY - 8, 8), :])
    pl.when(y_has_low)(now_low.start)
    pl.when(y_has_high)(now_high.start)

    def send_now(i, carry):
        chunk = order(i)
        band = pl.ds(pl.multiple_of(chunk * ROWS, 8), ROWS)
        low, high = x_copies(
            0, chunk, now_hbm.at[pl.ds(0, 4), band, :], now_hbm.at[pl.ds(4, 4), band, :]
        )
        pl.when(has_low)(low.start)
        pl.when(has_high)(high.start)
        return carry

    def trace_copy(peer, mine):
        return pltpu.make_async_remote_copy(
            src_ref=packed.at[peer],
            dst_ref=landed.at[mine],
            send_sem=trace_send.at[peer],
            recv_sem=trace_recv.at[mine],
            device_id={"gx": peer},
            device_id_type=MESH,
        )

    def send_traces(k, carry):
        trace_copy((gx + k) % NG, gx).start()
        return carry

    lax.fori_loop(1, NG, send_traces, 0)
    lax.fori_loop(0, CHUNKS, send_now, 0)

    landed[gx] = packed[gx]

    def wait_traces(k, carry):
        peer = (gx + k) % NG
        trace_copy(peer, peer).wait_recv()
        return carry

    lax.fori_loop(1, NG, wait_traces, 0)

    def wait_trace_sends(k, carry):
        peer = (gx + k) % NG
        trace_copy(peer, peer).wait_send()
        return carry

    lax.fori_loop(1, NG, wait_trace_sends, 0)

    arrived = landed[...].reshape(NG, 128)
    lane = iota((NG, 128), 1)
    spread = jnp.zeros((CY, 128), F32)
    for j in range(SLOTS):
        cell = arrived[:, 8 * j + STEPS : 8 * j + STEPS + 1].astype(jnp.int32)
        weights = jnp.zeros((NG, 128), F32)
        for t in range(STEPS):
            weights = jnp.where(lane // CX == t, arrived[:, 8 * j + t : 8 * j + t + 1], weights)
        weights = jnp.where(lane % CX == cell // CY, weights, 0.0)
        spot = jnp.where(lane == cell % CY, 1.0, 0.0)
        spread = spread + lax.dot_general(
            spot, weights, (((0,), (0,)), ((), ())), precision=HIGHEST, preferred_element_type=F32
        )
    at_depth = iota((CY, 128), 1) == ZREC
    for c in range(STEPS * CX):
        source[c] = jnp.where(at_depth, spread[:, c : c + 1], 0.0)

    for copy in loads:
        copy.wait()

    eight = iota((8, NZ), 0)

    def advance(t):
        now, later = t % 2, (t + 1) % 2

        def chunk_body(i, carry):
            chunk = order(i)
            low, high = x_field(now, chunk)
            pl.when(has_low)(high.wait_recv)
            pl.when(has_high)(low.wait_recv)
            if t >= 1:
                old_low, old_high = x_field(later, chunk)
                pl.when(has_low)(old_low.wait_send)
                pl.when(has_high)(old_high.wait_send)

            @pl.when(i == 0)
            def _():
                y_low, y_high = y_field(now)
                pl.when(y_has_low)(y_high.wait_recv)
                pl.when(y_has_high)(y_low.wait_recv)
                if t >= 1:
                    y_old_low, y_old_high = y_field(later)
                    pl.when(y_has_low)(y_old_low.wait_send)
                    pl.when(y_has_high)(y_old_high.wait_send)

            base = pl.multiple_of(chunk * ROWS, ROWS)
            depth[...] = jnp.dot(
                field[now, 4:12, pl.ds(base + 8, ROWS), :].reshape(CX * ROWS, NZ),
                table_ref[...],
                precision=HIGHEST,
                preferred_element_type=F32,
            ).reshape(CX, ROWS, NZ)

            def row_body(j, carry):
                top = pl.multiple_of(base + j * 16, 16)
                for x in range(CX):
                    wave = forward[t, x, pl.ds(top, 16), :].astype(F32)
                    for half in range(2):
                        inner = pl.multiple_of(j * 16 + half * 8, 8)
                        row = pl.multiple_of(top + half * 8, 8)
                        r = pl.ds(pl.multiple_of(row + 8, 8), 8)
                        mid = field[now, 4 + x, r, :]
                        above = field[now, 4 + x, pl.ds(row, 8), :]
                        below = field[now, 4 + x, pl.ds(pl.multiple_of(row + 16, 8), 8), :]
                        total_sum = depth[x, pl.ds(inner, 8), :]
                        for k, w in enumerate(coefficients, 1):
                            paired = field[now, 4 + x + k, r, :] + field[now, 4 + x - k, r, :]
                            paired += pltpu.roll(jnp.where(eight >= k, mid, below), 8 - k, 0)
                            paired += pltpu.roll(jnp.where(eight < 8 - k, mid, above), k, 0)
                            total_sum += w * paired
                        out_rows = pl.ds(row, 8)
                        following = (
                            2.0 * mid
                            - field[later, 4 + x, r, :]
                            + courant[x, out_rows, :] * total_sum
                        )
                        following = jnp.concatenate(
                            [
                                following[:, :128] + source[t * CX + x, out_rows, :],
                                following[:, 128:],
                            ],
                            axis=1,
                        )
                        field[later, 4 + x, r, :] = following
                        term = wave[half * 8 : half * 8 + 8] * following
                        if t == 0:
                            image[x, out_rows, :] = term
                        else:
                            image[x, out_rows, :] += term
                return carry

            lax.fori_loop(0, ROWS // 16, row_body, 0)

            if t < STEPS - 1:
                next_low, next_high = x_field(later, chunk)
                pl.when(has_low)(next_low.start)
                pl.when(has_high)(next_high.start)

                y_low, y_high = y_field(later)

                @pl.when(i == 0)
                def _():
                    pl.when(y_has_low)(y_low.start)

                @pl.when(i == 1)
                def _():
                    pl.when(y_has_high)(y_high.start)

            return carry

        lax.fori_loop(0, CHUNKS, chunk_body, 0)

    for t in range(STEPS):
        advance(t)

    store_last = pltpu.make_async_copy(
        field.at[STEPS % 2, pl.ds(4, CX), pl.ds(8, CY), :], last_hbm, store_sem.at[0]
    )
    store_image = pltpu.make_async_copy(image, image_hbm, store_sem.at[1])
    store_last.start()
    store_image.start()

    def weigh(j, carry):
        r = pl.ds(pl.multiple_of(j * 8, 8), 8)
        up = jnp.zeros((8, NZ), F32)
        down = jnp.zeros((8, NZ), F32)
        for x in range(CX):
            value = image[x, r, :]
            up += factor_ref[gx * CX + x] * value
            down += factor_ref[NG * CX + gx * CX + x] * value
        plane[0, r, :] = up
        plane[1, r, :] = down
        return carry

    lax.fori_loop(0, CY // 8, weigh, 0)

    def segment(q):
        return pl.ds(pl.multiple_of(q * SEG, SEG), SEG)

    def group_copy(peer, mine):
        return pltpu.make_async_remote_copy(
            src_ref=plane.at[:, segment(peer), :],
            dst_ref=group_in.at[mine],
            send_sem=group_send.at[peer],
            recv_sem=group_recv.at[mine],
            device_id={"gx": own_z * NQ + peer},
            device_id_type=MESH,
        )

    def line_copy(k):
        peer = (own_z + k) % NZD
        return pltpu.make_async_remote_copy(
            src_ref=total.at[(own_z + k) // NZD],
            dst_ref=line_in.at[own_z],
            send_sem=line_send.at[peer],
            recv_sem=line_recv.at[own_z],
            device_id={"gx": peer * NQ + own_q},
            device_id_type=MESH,
        )

    def line_arrival(k):
        peer = (own_z + k) % NZD
        return pltpu.make_async_remote_copy(
            src_ref=total.at[0],
            dst_ref=line_in.at[peer],
            send_sem=line_send.at[peer],
            recv_sem=line_recv.at[peer],
            device_id={"gx": peer * NQ + own_q},
            device_id_type=MESH,
        )

    def back_copy(peer, mine):
        return pltpu.make_async_remote_copy(
            src_ref=back.at[peer],
            dst_ref=sums.at[:, segment(mine), :],
            send_sem=back_send.at[peer],
            recv_sem=back_recv.at[mine],
            device_id={"gx": own_z * NQ + peer},
            device_id_type=MESH,
        )

    for k in range(1, NQ):
        group_copy((own_q + k) % NQ, own_q).start()
    group_in[own_q] = plane[:, segment(own_q), :]
    for k in range(1, NQ):
        peer = (own_q + k) % NQ
        group_copy(peer, peer).wait_recv()

    below_sum = group_in[0, 0]
    above_sum = group_in[NQ - 1, 1]
    for q in range(1, NQ):
        below_sum = below_sum + group_in[q, 0]
        above_sum = above_sum + group_in[NQ - 1 - q, 1]
    total[0] = below_sum
    total[1] = above_sum

    for k in range(1, NZD):
        line_copy(k).start()
    line_in[own_z] = jnp.zeros((SEG, NZ), F32)
    for k in range(1, NZD):
        line_arrival(k).wait_recv()

    low_sum = jnp.zeros((SEG, NZ), F32)
    high_sum = jnp.zeros((SEG, NZ), F32)
    for z in range(NZD):
        part = line_in[z]
        low_sum = low_sum + jnp.where(z < own_z, part, 0.0)
        high_sum = high_sum + jnp.where(z > own_z, part, 0.0)
    for q in range(NQ):
        back[q, 0] = low_sum
        low_sum = low_sum + group_in[q, 0]
        back[NQ - 1 - q, 1] = high_sum
        high_sum = high_sum + group_in[NQ - 1 - q, 1]

    for k in range(1, NQ):
        back_copy((own_q + k) % NQ, own_q).start()
    sums[:, segment(own_q), :] = back[own_q]
    for k in range(1, NQ):
        peer = (own_q + k) % NQ
        back_copy(peer, peer).wait_recv()

    store_sums = pltpu.make_async_copy(sums, sums_hbm, store_sem.at[2])
    store_sums.start()

    for k in range(1, NQ):
        peer = (own_q + k) % NQ
        group_copy(peer, peer).wait_send()
        back_copy(peer, peer).wait_send()
    for k in range(1, NZD):
        line_arrival(k).wait_send()
    def wait_sends(i, carry):
        low, high = x_field((STEPS - 1) % 2, i)
        pl.when(has_low)(low.wait_send)
        pl.when(has_high)(high.wait_send)
        return carry

    lax.fori_loop(0, CHUNKS, wait_sends, 0)
    low, high = y_field((STEPS - 1) % 2)
    pl.when(y_has_low)(low.wait_send)
    pl.when(y_has_high)(high.wait_send)
    store_last.wait()
    store_image.wait()
    store_sums.wait()


def update_kernel(
    factor_ref,
    image_ref,
    sums_ref,
    last_ref,
    courant_ref,
    first_ref,
    second_ref,
    courant_out,
    first_out,
    second_out,
    last_out,
):
    gx = lax.axis_index("gx")
    last_out[...] = last_ref[...]
    rows = image_ref.shape[1]

    def body(j, carry):
        r = pl.ds(pl.multiple_of(j * 8, 8), 8)
        low = sums_ref[0, r, :]
        high = sums_ref[1, r, :]
        values = [image_ref[x, r, :] for x in range(CX)]
        rise = [factor_ref[gx * CX + x] for x in range(CX)]
        fall = [factor_ref[NG * CX + gx * CX + x] for x in range(CX)]
        below = []
        for x in range(CX):
            low = low + rise[x] * values[x]
            below.append(low)
        for x in reversed(range(CX)):
            smoothed = fall[x] * below[x] + rise[x] * high
            high = high + fall[x] * values[x]
            first = beta_first * first_ref[x, r, :] + (1.0 - beta_first) * smoothed
            second = beta_second * second_ref[x, r, :] + (1.0 - beta_second) * smoothed * smoothed
            first_out[x, r, :] = first
            second_out[x, r, :] = second
            courant_out[x, r, :] = courant_ref[x, r, :] - learning_rate * (first / bias_first) / (
                jnp.sqrt(second / bias_second) + epsilon
            )
        return carry

    lax.fori_loop(0, rows // 8, body, 0)


def shards(
    courant,
    first_moment,
    second_moment,
    adjoint_prev,
    adjoint_now,
    forward_field,
    traces,
    trace_slab,
    trace_cell,
    trace_shot,
    rollback,
):
    factors = jnp.asarray(smoother_factors(NG * CX))
    table = jnp.asarray(depth_table())
    shape = jax.ShapeDtypeStruct((CX, CY, NZ), F32)
    anywhere = pl.BlockSpec(memory_space=pl.ANY)
    smem = pl.BlockSpec(memory_space=pltpu.SMEM)
    vmem = pl.BlockSpec(memory_space=pltpu.VMEM)
    dma = pltpu.SemaphoreType.DMA
    image, last, sums = pl.pallas_call(
        window_kernel,
        out_shape=(shape, shape, jax.ShapeDtypeStruct((2, CY, NZ), F32)),
        in_specs=[smem, smem, vmem, vmem, vmem, vmem, vmem] + [anywhere] * 4,
        out_specs=(anywhere,) * 3,
        scratch_shapes=[
            pltpu.VMEM((2, CX + 8, CY + 16, NZ), F32),
            pltpu.VMEM((CX, CY, NZ), F32),
            pltpu.VMEM((STEPS, CX, CY, NZ), jnp.bfloat16),
            pltpu.VMEM((CX, CY, NZ), F32),
            pltpu.VMEM((STEPS * CX, CY, 128), F32),
            pltpu.VMEM((NG, 1, 128), F32),
            pltpu.VMEM((NG, 1, 128), F32),
            pltpu.VMEM((CX, ROWS, NZ), F32),
            pltpu.VMEM((2, CY, NZ), F32),
            pltpu.VMEM((NQ, 2, SEG, NZ), F32),
            pltpu.VMEM((2, SEG, NZ), F32),
            pltpu.VMEM((NZD, SEG, NZ), F32),
            pltpu.VMEM((NQ, 2, SEG, NZ), F32),
            pltpu.VMEM((2, CY, NZ), F32),
            dma((4,)),
            dma((NG,)),
            dma((NG,)),
            dma((2, 2, CHUNKS)),
            dma((2, 2, CHUNKS)),
            dma((2, 2)),
            dma((2, 2)),
            dma((NQ,)),
            dma((NQ,)),
            dma((NZD,)),
            dma((NZD,)),
            dma((NQ,)),
            dma((NQ,)),
            dma((3,)),
        ],
        compiler_params=pltpu.CompilerParams(
            collective_id=0, has_side_effects=True, vmem_limit_bytes=24 << 20
        ),
    )(
        rollback,
        factors,
        table,
        traces,
        trace_slab,
        trace_cell,
        trace_shot,
        courant,
        adjoint_prev,
        adjoint_now,
        forward_field,
    )

    tile = 32
    block = pl.BlockSpec((CX, tile, NZ), lambda i: (0, i, 0))
    plane = pl.BlockSpec((2, tile, NZ), lambda i: (0, i, 0))
    return pl.pallas_call(
        update_kernel,
        grid=(CY // tile,),
        out_shape=(shape,) * 4,
        in_specs=[smem, block, plane, block, block, block, block],
        out_specs=(block,) * 4,
        compiler_params=pltpu.CompilerParams(vmem_limit_bytes=24 << 20),
    )(factors, image, sums, last, courant, first_moment, second_moment)


def solution(mesh):
    in_specs = (
        P("gx", "gy", None),
        P("gx", "gy", None),
        P("gx", "gy", None),
        P("gx", "gy", None),
        P("gx", "gy", None),
        P(None, "gx", "gy", None),
        P("gy", "gx", None),
        P("gy", "gx", None),
        P("gy", "gx"),
        P("gy", "gx"),
        P(),
    )
    out_specs = (P("gx", "gy", None),) * 4
    return jax.shard_map(shards, mesh=mesh, in_specs=in_specs, out_specs=out_specs, check_vma=False)
```

time: 213 us -> 77.9 us (0.37)
  starting transfers between devices: 74.6 us -> 0 us
  Pallas kernels: 0 us -> 66.4 us
  other arithmetic: 38.9 us -> 0 us
  blocking collectives: 34.2 us -> 0 us
  waiting for transfers between devices: 34 us -> 0 us
  local copies, waits for them, and re-layouts: 25.6 us -> 10.5 us
  matrix products: 3.33 us -> 0 us
    pallas_call x0 -> x2, Pallas kernels: none -> 66.4 us  [the longest x1 62.5 us: shards(): pl.pallas_call(window_kernel, out_shape=(shape, shape, jax.ShapeDtypeStru...]
    ppermute x16 -> x0, starting transfers between devices: 45.7 us -> none  [the longest x8 32.3 us: padded_2(): lax.ppermute(last, axis, up)]
    all_to_all x1 -> x0, blocking collectives: 34.2 us -> none  [shards(): lax.all_to_all(result, 'gx', split_axis=0, concat_axis=1, tiled=True)]
    all_to_all x2 -> x0, waiting for transfers between devices: 33.9 us -> none  [the longest x1 28.2 us: shards(): lax.all_to_all(gradient, 'gx', split_axis=1, concat_axis=0, tiled=True)]
    all_to_all x2 -> x0, starting transfers between devices: 28.9 us -> none  [the longest x1 16 us: shards(): lax.all_to_all(gradient, 'gx', split_axis=1, concat_axis=0, tiled=True)]
    add x9 -> x0, other arithmetic: 17.5 us -> none  [the longest x4 15.1 us: shards(): following = 2.0 * current - previous + courant * laplacian(current)]
    concatenate x8 -> x0, other arithmetic: 12.8 us -> none  [the longest x7 12.8 us: padded_2(): jnp.concatenate([jnp.pad(low, around), array, jnp.pad(high, around)], axi...]
    scatter-add x4 -> x0, local copies, waits for them, and re-layouts: 7.95 us -> none  [shards(): following = following.at[:, :, ZREC].add(source[step_index])]
  transfers between devices with their start and end apart: 18 -> 0, of which waited for: 2 -> 0; matrix products, arithmetic and copies ran while one was open for 4% -> 0% of each run, Pallas kernels for 0% -> 0%
where the time goes in v1:
time: 77.9 us; the launch traced here: 77.5 us
  Pallas kernels  66.4 us (85%)
  local copies, waits for them, and re-layouts  10.5 us (13%)
    pallas_call x1, Pallas kernels, shards(): pl.pallas_call(window_kernel, out_shape=(shape, shape, jax.ShapeDtypeStru...  62.5 us
    unnamed x27, local copies, waits for them, and re-layouts  10.5 us
    pallas_call x1, Pallas kernels, shards(): pl.pallas_call(update_kernel, grid=(CY // tile,), out_shape=(shape,) * 4,...  3.88 us

profile of v1, /device:TPU:1, one launch (start us, length us, event | category | flops | bytes accessed | tf_op | source)
XLA Modules:
  0.0 77.5 jit_solution(5653082330293176503)
XLA Ops:
  0.6 0.8 copy.17.slab_ref
  1.4 0.0 copy-start
  1.4 1.2 %copy-done = f32[8,128,256]{2,1,0:T(8,128)S(1)} copy-done((f32[8,128,256]{2,1,0:T(8,128)S(1)}, f32[8,128,256]{2,1,0:T(8,128)}, u32[]{:S(2)}) %copy-start) | copy-done | bytes 1048600
  2.6 0.0 copy-start.2
  2.6 1.6 %copy-done.2 = bf16[4,8,128,256]{3,2,1,0:T(8,128)(2,1)S(1)} copy-done((bf16[4,8,128,256]{3,2,1,0:T(8,128)(2,1)S(1)}, bf16[4,8,128,256]{3,2,1,0:T(8,128)(2,1)}, u32[]{:S(2)}) %copy-start.2) | copy-done | bytes 2097176
  4.2 0.0 copy-start.3
  4.2 1.2 %copy-done.3 = f32[8,128,256]{2,1,0:T(8,128)S(1)} copy-done((f32[8,128,256]{2,1,0:T(8,128)S(1)}, f32[8,128,256]{2,1,0:T(8,128)}, u32[]{:S(2)}) %copy-start.3) | copy-done | bytes 1048600
  5.4 0.0 copy-start.4
  5.4 1.2 %copy-done.4 = f32[8,128,256]{2,1,0:T(8,128)S(1)} copy-done((f32[8,128,256]{2,1,0:T(8,128)S(1)}, f32[8,128,256]{2,1,0:T(8,128)}, u32[]{:S(2)}) %copy-start.4) | copy-done | bytes 1048600
  6.7 0.0 copy-start.7
  6.7 0.9 %copy-done.7 = f32[256,256]{1,0:T(8,128)S(1)} copy-done((f32[256,256]{1,0:T(8,128)S(1)}, f32[256,256]{1,0:T(8,128)}, u32[]{:S(2)}) %copy-start.7) | copy-done | bytes 262168
  7.6 0.0 copy-start.8
  7.6 0.8 %copy-done.8 = f32[1,128,128]{2,1,0:T(8,128)S(1)} copy-done((f32[1,128,128]{2,1,0:T(8,128)S(1)}, f32[1,128,128]{2,1,0:T(8,128)}, u32[]{:S(2)}) %copy-start.8) | copy-done | bytes 65560
  8.5 0.0 copy-start.9
  8.5 0.7 copy-done.9
  9.1 0.0 copy-start.10
  9.1 0.7 copy-done.10
  9.8 0.0 copy-start.11
  9.8 0.7 copy-done.11
  10.4 0.0 copy-start.12
  10.5 0.7 copy-done.12
  11.1 0.0 copy-start.1
  11.1 0.0 copy-start.5
  11.1 0.0 copy-start.6
  11.1 62.5 %shard_map.156 = (f32[8,128,256]{2,1,0:T(8,128)S(1)}, f32[8,128,256]{2,1,0:T(8,128)S(1)}, f32[2,128,256]{2,1,0:T(8,128)S(1)}) custom-call(s32[16]{0:T(128)S(1)} %copy-done.10, f32[1024]{0:T(1024)S(1)} %copy-done.9, f32[256,256]{1,0:T(8,128)S(1)} %copy-done.7, f32[1,128,128]{2,1,0:T(8,128)S(1)} %copy-done.8, s32[1,128,1]{2,1,0:T(8,128)S(1)} %copy.17.slab_ref, ...), custom_call_target="tpu_custom_call" | custom-call | tf_op jit(solution)/shard_map/pallas_call | solution.py:600
  73.6 0.0 copy-done.1
  73.6 0.0 copy-done.5
  73.7 0.0 copy-done.6
  73.7 3.9 %shard_map.157 = (f32[8,128,256]{2,1,0:T(8,128)}, f32[8,128,256]{2,1,0:T(8,128)}, f32[8,128,256]{2,1,0:T(8,128)}, f32[8,128,256]{2,1,0:T(8,128)}) custom-call(f32[1024]{0:T(1024)S(1)} %copy-done.9, f32[8,128,256]{2,1,0:T(8,128)S(1)} %get-tuple-element.7.image_ref, f32[2,128,256]{2,1,0:T(8,128)S(1)} %get-tuple-element.8.sums_ref, ...), custom_call_target="tpu_custom_call" | custom-call | tf_op jit(solution)/shard_map/pallas_call | solution.py:655
Async XLA Ops:
  1.4 1.2 %copy-start = (f32[8,128,256]{2,1,0:T(8,128)S(1)}, f32[8,128,256]{2,1,0:T(8,128)}, u32[]{:S(2)}) copy-start(f32[8,128,256]{2,1,0:T(8,128)} %courant_ref.1) | copy-start | bytes 3145732
  2.6 1.6 %copy-start.2 = (bf16[4,8,128,256]{3,2,1,0:T(8,128)(2,1)S(1)}, bf16[4,8,128,256]{3,2,1,0:T(8,128)(2,1)}, u32[]{:S(2)}) copy-start(bf16[4,8,128,256]{3,2,1,0:T(8,128)(2,1)} %forward_hbm.1) | copy-start | bytes 6291460
  4.2 1.2 %copy-start.3 = (f32[8,128,256]{2,1,0:T(8,128)S(1)}, f32[8,128,256]{2,1,0:T(8,128)}, u32[]{:S(2)}) copy-start(f32[8,128,256]{2,1,0:T(8,128)} %prev_hbm.1) | copy-start | bytes 3145732
  5.4 1.2 %copy-start.4 = (f32[8,128,256]{2,1,0:T(8,128)S(1)}, f32[8,128,256]{2,1,0:T(8,128)}, u32[]{:S(2)}) copy-start(f32[8,128,256]{2,1,0:T(8,128)} %now_hbm.1) | copy-start | bytes 3145732
  6.7 0.9 %copy-start.7 = (f32[256,256]{1,0:T(8,128)S(1)}, f32[256,256]{1,0:T(8,128)}, u32[]{:S(2)}) copy-start(f32[256,256]{1,0:T(8,128)} %constant.5.clone.table_ref) | copy-start | bytes 786436
  7.6 0.8 %copy-start.8 = (f32[1,128,128]{2,1,0:T(8,128)S(1)}, f32[1,128,128]{2,1,0:T(8,128)}, u32[]{:S(2)}) copy-start(f32[1,128,128]{2,1,0:T(8,128)} %traces_ref.1) | copy-start | bytes 196612
  8.5 0.7 copy-start.9
  9.1 0.7 copy-start.10
  9.8 0.7 copy-start.11
  10.4 0.7 copy-start.12
  11.1 62.5 %copy-start.1 = (f32[8,128,256]{2,1,0:T(8,128)S(1)}, f32[8,128,256]{2,1,0:T(8,128)}, u32[]{:S(2)}) copy-start(f32[8,128,256]{2,1,0:T(8,128)} %courant_ref.1) | copy-start | bytes 3145732
  11.1 62.5 %copy-start.5 = (f32[8,128,256]{2,1,0:T(8,128)S(1)}, f32[8,128,256]{2,1,0:T(8,128)}, u32[]{:S(2)}) copy-start(f32[8,128,256]{2,1,0:T(8,128)} %first_ref.1) | copy-start | bytes 3145732
  11.1 62.6 %copy-start.6 = (f32[8,128,256]{2,1,0:T(8,128)S(1)}, f32[8,128,256]{2,1,0:T(8,128)}, u32[]{:S(2)}) copy-start(f32[8,128,256]{2,1,0:T(8,128)} %second_ref.1) | copy-start | bytes 3145732

commit v2 on v1

--- a/solution.py
+++ b/solution.py
@@ -25,6 +25,7 @@
 SLOTS = 4
 ROWS = 32
 CHUNKS = CY // ROWS
+UPDATE_ROWS = 32
 SEG = CY // NQ
 
 coefficients = (8.0 / 5.0, -1.0 / 5.0, 8.0 / 315.0, -1.0 / 560.0)
@@ -65,6 +66,20 @@
 
 
 def window_kernel(
+    rollback_hbm,
+    factor_hbm,
+    table_hbm,
+    traces_hbm,
+    slab_hbm,
+    cell_hbm,
+    shot_hbm,
+    courant_hbm,
+    prev_hbm,
+    now_hbm,
+    forward_hbm,
+    image_hbm,
+    last_hbm,
+    sums_hbm,
     rollback_ref,
     factor_ref,
     table_ref,
@@ -72,13 +87,6 @@
     slab_ref,
     cell_ref,
     shot_ref,
-    courant_hbm,
-    prev_hbm,
-    now_hbm,
-    forward_hbm,
-    image_hbm,
-    last_hbm,
-    sums_hbm,
     field,
     courant,
     forward,
@@ -113,6 +121,22 @@
     own_z = gx // NQ
     own_q = gx % NQ
 
+    small = [
+        pltpu.make_async_copy(source_ref, target_ref, load_sem.at[4 + k])
+        for k, (source_ref, target_ref) in enumerate(
+            (
+                (traces_hbm, traces_ref),
+                (slab_hbm, slab_ref),
+                (cell_hbm, cell_ref),
+                (shot_hbm, shot_ref),
+                (rollback_hbm, rollback_ref),
+                (table_hbm, table_ref),
+                (factor_hbm, factor_ref),
+            )
+        )
+    ]
+    for copy in small:
+        copy.start()
     loads = [
         pltpu.make_async_copy(
             now_hbm, field.at[0, pl.ds(4, CX), pl.ds(8, CY), :], load_sem.at[0]
@@ -156,10 +180,13 @@
             barrier, inc=1, device_id={"gy": (gy + k) % NYD}, device_id_type=MESH
         )
 
+    for copy in small[:5]:
+        copy.wait()
+
     rows = iota((BLOCKS, 128), 0)
     lanes = iota((BLOCKS, 128), 1)
     diagonal = rows == lanes
-    slab_col = slab_ref[0]
+    slab_float = slab_ref[...].astype(F32)
     shot_row = shot_ref[...]
     cell_row = cell_ref[...].astype(F32)
     live_row = jnp.zeros((1, 128), F32)
@@ -168,10 +195,10 @@
         live_row = jnp.where(shot_row == s, flag, live_row)
     live_col = jnp.sum(jnp.where(diagonal, live_row, 0.0), axis=1, keepdims=True)
     cell_col = jnp.sum(jnp.where(diagonal, cell_row, 0.0), axis=1, keepdims=True)
-    slab_float = slab_col.astype(F32)
-    slab_row = jnp.sum(jnp.where(diagonal, slab_float, 0.0), axis=0, keepdims=True)
+    slab_row = slab_float
+    slab_col = jnp.sum(jnp.where(diagonal, slab_row, 0.0), axis=1, keepdims=True)
     slot_col = jnp.sum(
-        jnp.where((slab_float == slab_row) & (lanes < rows), 1.0, 0.0), axis=1, keepdims=True
+        jnp.where((slab_col == slab_row) & (lanes < rows), 1.0, 0.0), axis=1, keepdims=True
     )
     pick = jnp.where((lanes % 8 == rows // SAMPLES_PER_STEP) & (lanes < 8 * SLOTS), 1.0, 0.0)
     reduced = jnp.dot(traces_ref[0], pick, precision=HIGHEST, preferred_element_type=F32)
@@ -306,7 +333,7 @@
     for c in range(STEPS * CX):
         source[c] = jnp.where(at_depth, spread[:, c : c + 1], 0.0)
 
-    for copy in loads:
+    for copy in loads + small[5:]:
         copy.wait()
 
     eight = iota((8, NZ), 0)
@@ -546,35 +573,52 @@
     first_out,
     second_out,
     last_out,
+    fresh,
+    store_sem,
 ):
     gx = lax.axis_index("gx")
-    last_out[...] = last_ref[...]
-    rows = image_ref.shape[1]
-
-    def body(j, carry):
-        r = pl.ds(pl.multiple_of(j * 8, 8), 8)
-        low = sums_ref[0, r, :]
-        high = sums_ref[1, r, :]
-        values = [image_ref[x, r, :] for x in range(CX)]
-        rise = [factor_ref[gx * CX + x] for x in range(CX)]
-        fall = [factor_ref[NG * CX + gx * CX + x] for x in range(CX)]
-        below = []
-        for x in range(CX):
-            low = low + rise[x] * values[x]
-            below.append(low)
-        for x in reversed(range(CX)):
-            smoothed = fall[x] * below[x] + rise[x] * high
-            high = high + fall[x] * values[x]
-            first = beta_first * first_ref[x, r, :] + (1.0 - beta_first) * smoothed
-            second = beta_second * second_ref[x, r, :] + (1.0 - beta_second) * smoothed * smoothed
-            first_out[x, r, :] = first
-            second_out[x, r, :] = second
-            courant_out[x, r, :] = courant_ref[x, r, :] - learning_rate * (first / bias_first) / (
-                jnp.sqrt(second / bias_second) + epsilon
-            )
-        return carry
-
-    lax.fori_loop(0, rows // 8, body, 0)
+    store_last = pltpu.make_async_copy(last_ref, last_out, store_sem.at[3, 0])
+    store_last.start()
+    rise = [factor_ref[gx * CX + x] for x in range(CX)]
+    fall = [factor_ref[NG * CX + gx * CX + x] for x in range(CX)]
+
+    def stores(part):
+        band = pl.ds(part * UPDATE_ROWS, UPDATE_ROWS)
+        return [
+            pltpu.make_async_copy(fresh.at[k, :, band, :], out.at[:, band, :], store_sem.at[k, part])
+            for k, out in enumerate((courant_out, first_out, second_out))
+        ]
+
+    for part in range(CY // UPDATE_ROWS):
+
+        def body(j, carry):
+            r = pl.ds(pl.multiple_of(part * UPDATE_ROWS + j * 8, 8), 8)
+            low = sums_ref[0, r, :]
+            high = sums_ref[1, r, :]
+            values = [image_ref[x, r, :] for x in range(CX)]
+            below = []
+            for x in range(CX):
+                low = low + rise[x] * values[x]
+                below.append(low)
+            for x in reversed(range(CX)):
+                smoothed = fall[x] * below[x] + rise[x] * high
+                high = high + fall[x] * values[x]
+                first = beta_first * first_ref[x, r, :] + (1.0 - beta_first) * smoothed
+                second = beta_second * second_ref[x, r, :] + (1.0 - beta_second) * smoothed * smoothed
+                fresh[1, x, r, :] = first
+                fresh[2, x, r, :] = second
+                fresh[0, x, r, :] = courant_ref[x, r, :] - learning_rate * (first / bias_first) / (
+                    jnp.sqrt(second / bias_second) + epsilon
+                )
+            return carry
+
+        lax.fori_loop(0, UPDATE_ROWS // 8, body, 0)
+        for copy in stores(part):
+            copy.start()
+    for part in range(CY // UPDATE_ROWS):
+        for copy in stores(part):
+            copy.wait()
+    store_last.wait()
 
 
 def shards(
@@ -594,15 +638,23 @@
     table = jnp.asarray(depth_table())
     shape = jax.ShapeDtypeStruct((CX, CY, NZ), F32)
     anywhere = pl.BlockSpec(memory_space=pl.ANY)
+    hbm = pl.BlockSpec(memory_space=pltpu.HBM)
     smem = pl.BlockSpec(memory_space=pltpu.SMEM)
     vmem = pl.BlockSpec(memory_space=pltpu.VMEM)
     dma = pltpu.SemaphoreType.DMA
     image, last, sums = pl.pallas_call(
         window_kernel,
         out_shape=(shape, shape, jax.ShapeDtypeStruct((2, CY, NZ), F32)),
-        in_specs=[smem, smem, vmem, vmem, vmem, vmem, vmem] + [anywhere] * 4,
+        in_specs=[hbm] * 11,
         out_specs=(anywhere,) * 3,
         scratch_shapes=[
+            pltpu.SMEM((SHOTS,), jnp.int32),
+            pltpu.SMEM((2 * NG * CX,), F32),
+            pltpu.VMEM((NZ, NZ), F32),
+            pltpu.VMEM((1, BLOCKS, 128), F32),
+            pltpu.VMEM((1, BLOCKS), jnp.int32),
+            pltpu.VMEM((1, BLOCKS), jnp.int32),
+            pltpu.VMEM((1, BLOCKS), jnp.int32),
             pltpu.VMEM((2, CX + 8, CY + 16, NZ), F32),
             pltpu.VMEM((CX, CY, NZ), F32),
             pltpu.VMEM((STEPS, CX, CY, NZ), jnp.bfloat16),
@@ -617,7 +669,7 @@
             pltpu.VMEM((NZD, SEG, NZ), F32),
             pltpu.VMEM((NQ, 2, SEG, NZ), F32),
             pltpu.VMEM((2, CY, NZ), F32),
-            dma((4,)),
+            dma((11,)),
             dma((NG,)),
             dma((NG,)),
             dma((2, 2, CHUNKS)),
@@ -636,28 +688,30 @@
             collective_id=0, has_side_effects=True, vmem_limit_bytes=24 << 20
         ),
     )(
-        rollback,
-        factors,
-        table,
-        traces,
-        trace_slab,
-        trace_cell,
-        trace_shot,
-        courant,
-        adjoint_prev,
-        adjoint_now,
-        forward_field,
+        *(
+            pltpu.with_memory_space_constraint(operand, pltpu.HBM)
+            for operand in (
+                rollback,
+                factors,
+                table,
+                traces,
+                trace_slab.reshape(1, BLOCKS),
+                trace_cell,
+                trace_shot,
+                courant,
+                adjoint_prev,
+                adjoint_now,
+                forward_field,
+            )
+        )
     )
 
-    tile = 32
-    block = pl.BlockSpec((CX, tile, NZ), lambda i: (0, i, 0))
-    plane = pl.BlockSpec((2, tile, NZ), lambda i: (0, i, 0))
     return pl.pallas_call(
         update_kernel,
-        grid=(CY // tile,),
         out_shape=(shape,) * 4,
-        in_specs=[smem, block, plane, block, block, block, block],
-        out_specs=(block,) * 4,
+        in_specs=[smem] + [vmem] * 6,
+        out_specs=(anywhere,) * 4,
+        scratch_shapes=[pltpu.VMEM((3, CX, CY, NZ), F32), dma((4, CY // UPDATE_ROWS))],
         compiler_params=pltpu.CompilerParams(vmem_limit_bytes=24 << 20),
     )(factors, image, sums, last, courant, first_moment, second_moment)
 

time: 77.9 us -> 65.5 us (0.84)
  local copies, waits for them, and re-layouts: 10.5 us -> 0.02 us
  Pallas kernels: 66.4 us -> 64.7 us
    unnamed x27 -> x8, local copies, waits for them, and re-layouts: 10.5 us -> 0.02 us
    pallas_call x1, Pallas kernels: 3.88 us -> 2.92 us  [shards(): pl.pallas_call(update_kernel, out_shape=(shape,) * 4, in_specs=[smem] + [...]
where the time goes in v2:
time: 65.5 us; the launch traced here: 65.4 us
  Pallas kernels  64.7 us (99%)
  between operations  0.71 us (1%)
    pallas_call x1, Pallas kernels, shards(): pl.pallas_call(window_kernel, out_shape=(shape, shape, jax.ShapeDtypeStru...  61.8 us
    pallas_call x1, Pallas kernels, shards(): pl.pallas_call(update_kernel, out_shape=(shape,) * 4, in_specs=[smem] + [...  2.92 us

profile of v2, /device:TPU:1, one launch (start us, length us, event | category | flops | bytes accessed | tf_op | source)
XLA Modules:
  0.0 65.4 jit_solution(14849449337931541851)
XLA Ops:
  0.6 0.0 copy-start
  0.6 0.0 copy-start.1
  0.7 0.0 copy-start.2
  0.7 0.0 copy-start.3
  0.7 61.8 %shard_map.156 = (f32[8,128,256]{2,1,0:T(8,128)S(1)}, f32[8,128,256]{2,1,0:T(8,128)S(1)}, f32[2,128,256]{2,1,0:T(8,128)S(1)}) custom-call(s32[16]{0:T(128)} %rollback_hbm.1, f32[1024]{0:T(1024)} %constant.4.clone.factor_hbm.factor_ref, f32[256,256]{1,0:T(8,128)} %constant.5.clone.table_hbm, f32[1,128,128]{2,1,0:T(8,128)} %traces_hbm.1, s32[1,128]{1,0:T(1,128)} %bitcast.1, ...), custom_call_target="tpu_custom_call" | custom-call | tf_op jit(solution)/shard_map/pallas_call | solution.py:645
  62.5 0.0 copy-done
  62.5 0.0 copy-done.1
  62.5 0.0 copy-done.2
  62.5 0.0 copy-done.3
  62.5 2.9 %shard_map.157 = (f32[8,128,256]{2,1,0:T(8,128)}, f32[8,128,256]{2,1,0:T(8,128)}, f32[8,128,256]{2,1,0:T(8,128)}, f32[8,128,256]{2,1,0:T(8,128)}) custom-call(f32[1024]{0:T(1024)S(1)} %copy-done.3, f32[8,128,256]{2,1,0:T(8,128)S(1)} %get-tuple-element.7.image_ref, f32[2,128,256]{2,1,0:T(8,128)S(1)} %get-tuple-element.8.sums_ref, ...), custom_call_target="tpu_custom_call" | custom-call | tf_op jit(solution)/shard_map/pallas_call | solution.py:709
Async XLA Ops:
  0.6 61.8 %copy-start = (f32[8,128,256]{2,1,0:T(8,128)S(1)}, f32[8,128,256]{2,1,0:T(8,128)}, u32[]{:S(2)}) copy-start(f32[8,128,256]{2,1,0:T(8,128)} %courant_ref.1) | copy-start | bytes 3145732
  0.6 61.8 %copy-start.1 = (f32[8,128,256]{2,1,0:T(8,128)S(1)}, f32[8,128,256]{2,1,0:T(8,128)}, u32[]{:S(2)}) copy-start(f32[8,128,256]{2,1,0:T(8,128)} %first_ref.1) | copy-start | bytes 3145732
  0.7 61.8 %copy-start.2 = (f32[8,128,256]{2,1,0:T(8,128)S(1)}, f32[8,128,256]{2,1,0:T(8,128)}, u32[]{:S(2)}) copy-start(f32[8,128,256]{2,1,0:T(8,128)} %second_ref.1) | copy-start | bytes 3145732
  0.7 61.8 %copy-start.3 = (f32[1024]{0:T(1024)S(1)}, f32[1024]{0:T(1024)}, u32[]{:S(2)}) copy-start(f32[1024]{0:T(1024)} %constant.4.clone.factor_hbm.factor_ref) | copy-start | bytes 12292

commit v3 on v2

v3 whole, which is shorter than its diff:
```python
import math

import jax
import jax.numpy as jnp
import numpy as np
from jax import lax
from jax.experimental import pallas as pl
from jax.experimental.pallas import tpu as pltpu
from jax.sharding import PartitionSpec as P

MESH = pl.DeviceIdType.MESH
F32 = jnp.float32
HIGHEST = lax.Precision.HIGHEST

STEPS = 4
SAMPLES_PER_STEP = 32
ZREC = 8
SHOTS = 16
NG = 64
NYD = 4
NQ = 8
NZD = 8
CX, CY, NZ = 8, 128, 256
BLOCKS = 128
SLOTS = 4
ROWS = 16
CHUNKS = CY // ROWS
GROUP = 32 // ROWS
BATCHES = CHUNKS // GROUP
PASS_AFTER = 2
FAR_FIRST = (4, 3, 5, 2, 6, 7, 1)
UPDATE_ROWS = 32

coefficients = (8.0 / 5.0, -1.0 / 5.0, 8.0 / 315.0, -1.0 / 560.0)
center_weight = -205.0 / 72.0
smooth_length = 4096.0
cosh_value = 1.0 + 0.5 / smooth_length
theta = math.log(cosh_value + math.sqrt(cosh_value * cosh_value - 1.0))
image_gain = 10.0
beta_first = 0.9
beta_second = 0.999
bias_first = 1.0 - 0.9**10
bias_second = 1.0 - 0.999**10
learning_rate = 0.01
epsilon = 1e-08


def depth_table():
    table = np.zeros((NZ, NZ), np.float64)
    for i in range(NZ):
        for k, w in enumerate(coefficients, 1):
            if i + k < NZ:
                table[i + k, i] = w
                table[i, i + k] = w
    table = jnp.asarray(table.astype(np.float32))
    high = table.astype(jnp.bfloat16)
    return jnp.stack([high, (table - high.astype(F32)).astype(jnp.bfloat16)])


def smoother_factors(count):
    position = np.arange(count, dtype=np.float64)
    scale = math.sqrt(image_gain / (smooth_length * math.sinh(theta) * math.sinh(theta * (count + 1))))
    rise = scale * np.sinh(theta * (position + 1.0))
    fall = scale * np.sinh(theta * (count - position))
    return np.concatenate([rise, fall]).astype(np.float32)


def iota(shape, dim):
    return lax.broadcasted_iota(jnp.int32, shape, dim)


def window_kernel(
    rollback_hbm,
    factor_hbm,
    table_hbm,
    traces_hbm,
    slab_hbm,
    cell_hbm,
    shot_hbm,
    courant_hbm,
    prev_hbm,
    now_hbm,
    forward_hbm,
    image_hbm,
    last_hbm,
    sums_hbm,
    rollback_ref,
    factor_ref,
    table_ref,
    traces_ref,
    slab_ref,
    cell_ref,
    shot_ref,
    field,
    courant,
    forward,
    image,
    source,
    packed,
    passed,
    landed,
    depth,
    plane,
    group_in,
    total,
    line_in,
    back,
    load_sem,
    known_sem,
    pack_send,
    pack_recv,
    pass_send,
    pass_recv,
    x_send,
    x_recv,
    y_send,
    y_recv,
    x_half_send,
    x_half_recv,
    y_half_send,
    y_half_recv,
    group_send,
    group_recv,
    line_send,
    line_recv,
    back_send,
    back_recv,
    store_sem,
):
    gx = lax.axis_index("gx")
    gy = lax.axis_index("gy")
    own_z = gx // NQ
    own_q = gx % NQ

    def at_group(q):
        return {"gx": own_z * NQ + q}

    def at_line(z):
        return {"gx": z * NQ + own_q}

    def remote(source_ref, target_ref, send_sem, recv_sem, device):
        return pltpu.make_async_remote_copy(
            src_ref=source_ref,
            dst_ref=target_ref,
            send_sem=send_sem,
            recv_sem=recv_sem,
            device_id=device,
            device_id_type=MESH,
        )

    def signal(sem, device):
        pl.semaphore_signal(sem, inc=1, device_id=device, device_id_type=MESH)

    barrier = pltpu.get_barrier_semaphore()
    at_edge = own_q % (NQ - 1) == 0
    for k in range(1, NQ):
        signal(barrier, at_group((own_q + k) % NQ))
    for k in (1, NYD - 1):
        signal(barrier, {"gy": (gy + k) % NYD})
    for k in (1, NZD - 1):
        signal(barrier, at_line((own_z + k) % NZD))
    across = (gx + 1 - 2 * ((NQ - 1 - own_q) // (NQ - 1)) + NG) % NG

    @pl.when(at_edge)
    def _():
        signal(barrier, {"gx": across})

    small = [
        pltpu.make_async_copy(source_ref, target_ref, load_sem.at[4 + k])
        for k, (source_ref, target_ref) in enumerate(
            (
                (traces_hbm, traces_ref),
                (slab_hbm, slab_ref),
                (cell_hbm, cell_ref),
                (shot_hbm, shot_ref),
                (rollback_hbm, rollback_ref),
                (table_hbm, table_ref),
                (factor_hbm, factor_ref),
            )
        )
    ]
    for copy in small:
        copy.start()
    loads = [
        pltpu.make_async_copy(
            now_hbm, field.at[0, pl.ds(4, CX), pl.ds(8, CY), :], load_sem.at[0]
        ),
        pltpu.make_async_copy(
            prev_hbm, field.at[1, pl.ds(4, CX), pl.ds(8, CY), :], load_sem.at[1]
        ),
        pltpu.make_async_copy(courant_hbm, courant, load_sem.at[2]),
        pltpu.make_async_copy(forward_hbm, forward, load_sem.at[3]),
    ]
    for copy in loads:
        copy.start()

    @pl.when(gx == 0)
    def _():
        field[:, 0:4, 8 : 8 + CY, :] = jnp.zeros((2, 4, CY, NZ), F32)

    @pl.when(gx == NG - 1)
    def _():
        field[:, 12:16, 8 : 8 + CY, :] = jnp.zeros((2, 4, CY, NZ), F32)

    @pl.when(gy == 0)
    def _():
        field[:, 4:12, 0:8, :] = jnp.zeros((2, CX, 8, NZ), F32)

    @pl.when(gy == NYD - 1)
    def _():
        field[:, 4:12, 8 + CY : 16 + CY, :] = jnp.zeros((2, CX, 8, NZ), F32)

    pl.semaphore_wait(barrier, NQ - 1 + 4 + 1 - (own_q % (NQ - 1) + NQ - 2) // (NQ - 1))

    has_low, has_high = gx > 0, gx < NG - 1
    y_has_low, y_has_high = gy > 0, gy < NYD - 1
    x_low = {"gx": (gx + NG - 1) % NG}
    x_high = {"gx": (gx + 1) % NG}
    y_low = {"gy": (gy + NYD - 1) % NYD}
    y_high = {"gy": (gy + 1) % NYD}
    every = pl.ds(0, NZ)

    def order(i):
        return (CHUNKS - i) % CHUNKS

    def band_of(chunk, start):
        return pl.ds(pl.multiple_of(start + chunk * ROWS, 8), ROWS)

    def x_pair(parity, chunk, sources, lanes, send, recv):
        band = band_of(chunk, 8)
        low = remote(
            sources[0], field.at[parity, pl.ds(12, 4), band, lanes], send(0), recv(1), x_low
        )
        high = remote(
            sources[1], field.at[parity, pl.ds(0, 4), band, lanes], send(1), recv(0), x_high
        )
        return low, high

    def x_field(parity, chunk, half=None):
        band = band_of(chunk, 8)
        if half is None:
            lanes = every
            send = lambda side: x_send.at[parity, side, chunk]
            recv = lambda side: x_recv.at[parity, side, chunk]
        else:
            lanes = pl.ds(half * 128, 128)
            send = lambda side: x_half_send.at[half, side, chunk]
            recv = lambda side: x_half_recv.at[half, side, chunk]
        sources = (
            field.at[parity, pl.ds(4, 4), band, lanes],
            field.at[parity, pl.ds(8, 4), band, lanes],
        )
        return x_pair(parity, chunk, sources, lanes, send, recv)

    def y_pair(parity, sources, lanes, send, recv):
        low = remote(
            sources[0],
            field.at[parity, pl.ds(4, CX), pl.ds(8 + CY, 8), lanes],
            send(0),
            recv(1),
            y_low,
        )
        high = remote(
            sources[1], field.at[parity, pl.ds(4, CX), pl.ds(0, 8), lanes], send(1), recv(0), y_high
        )
        return low, high

    def y_field(parity, half=None):
        if half is None:
            lanes = every
            send = lambda side: y_send.at[parity, side]
            recv = lambda side: y_recv.at[parity, side]
        else:
            lanes = pl.ds(half * 128, 128)
            send = lambda side: y_half_send.at[half, side]
            recv = lambda side: y_half_recv.at[half, side]
        sources = (
            field.at[parity, pl.ds(4, CX), pl.ds(8, 8), lanes],
            field.at[parity, pl.ds(4, CX), pl.ds(CY, 8), lanes],
        )
        return y_pair(parity, sources, lanes, send, recv)

    low, high = y_pair(
        0,
        (now_hbm.at[:, pl.ds(0, 8), :], now_hbm.at[:, pl.ds(CY - 8, 8), :]),
        every,
        lambda side: y_send.at[0, side],
        lambda side: y_recv.at[0, side],
    )
    pl.when(y_has_low)(low.start)
    pl.when(y_has_high)(high.start)

    def send_now(i, carry):
        chunk = order(i)
        band = band_of(chunk, 0)
        low, high = x_pair(
            0,
            chunk,
            (now_hbm.at[pl.ds(0, 4), band, :], now_hbm.at[pl.ds(4, 4), band, :]),
            every,
            lambda side: x_send.at[0, side, chunk],
            lambda side: x_recv.at[0, side, chunk],
        )
        pl.when(has_low)(low.start)
        pl.when(has_high)(high.start)
        return carry

    send_now(0, 0)

    line_next = at_line((own_z + 1) % NZD)
    line_prev = at_line((own_z + NZD - 1) % NZD)
    signal(known_sem.at[0, 0], line_next)
    signal(known_sem.at[1, 0], line_prev)

    for copy in small[:5]:
        copy.wait()
    rows = iota((BLOCKS, 128), 0)
    lanes = iota((BLOCKS, 128), 1)
    diagonal = rows == lanes
    slab_row = slab_ref[...].astype(F32)
    shot_row = shot_ref[...]
    cell_row = cell_ref[...].astype(F32)
    live_row = jnp.zeros((1, 128), F32)
    for s in range(SHOTS):
        flag = jnp.where(rollback_ref[s] == 0, 1.0, 0.0)
        live_row = jnp.where(shot_row == s, flag, live_row)
    live_col = jnp.sum(jnp.where(diagonal, live_row, 0.0), axis=1, keepdims=True)
    cell_col = jnp.sum(jnp.where(diagonal, cell_row, 0.0), axis=1, keepdims=True)
    slab_col = jnp.sum(jnp.where(diagonal, slab_row, 0.0), axis=1, keepdims=True)
    slot_col = jnp.sum(
        jnp.where((slab_col == slab_row) & (lanes < rows), 1.0, 0.0), axis=1, keepdims=True
    )
    pick = jnp.where((lanes % 8 == rows // SAMPLES_PER_STEP) & (lanes < 8 * SLOTS), 1.0, 0.0)
    reduced = jnp.dot(traces_ref[0], pick, precision=HIGHEST, preferred_element_type=F32)
    entries = reduced * live_col + jnp.where(lanes % 8 == STEPS, cell_col, 0.0)
    entries = jnp.where(slot_col == (lanes // 8).astype(F32), entries, 0.0)
    row = iota((NG, BLOCKS), 0)
    row_slab = (row % NZD) * NQ + row // NZD
    named = jnp.where(row_slab.astype(F32) == slab_row, 1.0, 0.0)
    packed[...] = jnp.dot(
        named, entries, precision=HIGHEST, preferred_element_type=F32
    ).reshape(NQ, NZD, 1, 128)

    def pack_copy(peer, mine):
        return remote(
            packed.at[peer], passed.at[mine], pack_send.at[peer], pack_recv.at[mine], at_group(peer)
        )

    def pass_copy(peer, mine):
        return remote(
            passed.at[:, peer], landed.at[mine], pass_send.at[peer], pass_recv.at[mine], at_line(peer)
        )

    for k in FAR_FIRST:
        pack_copy((own_q + k) % NQ, own_q).start()
    lax.fori_loop(1, CHUNKS, send_now, 0)
    passed[own_q] = packed[own_q]

    pl.semaphore_wait(known_sem.at[0, 0], 1)
    signal(known_sem.at[0, 1], line_next)
    pl.semaphore_wait(known_sem.at[1, 0], 1)
    signal(known_sem.at[1, 1], line_prev)
    pl.semaphore_wait(known_sem.at[0, 1], 1)
    signal(known_sem.at[0, 2], line_next)
    pl.semaphore_wait(known_sem.at[1, 1], 1)
    pl.semaphore_wait(known_sem.at[0, 2], 1)

    def pass_on():
        for k in range(1, NQ):
            peer = (own_q + k) % NQ
            pack_copy(peer, peer).wait_recv()
        for k in FAR_FIRST:
            pass_copy((own_z + k) % NZD, own_z).start()
        landed[own_z] = passed[:, own_z]

    for copy in loads + small[5:]:
        copy.wait()

    eight = iota((8, NZ), 0)
    at_depth = iota((8, 128), 1) == ZREC
    rise = [factor_ref[gx * CX + x] for x in range(CX)]
    fall = [factor_ref[NG * CX + gx * CX + x] for x in range(CX)]

    def group_copy(chunk, peer, mine):
        return remote(
            plane.at[chunk, peer],
            group_in.at[chunk, mine],
            group_send.at[chunk, peer],
            group_recv.at[chunk, mine],
            at_group(peer),
        )

    def line_copy(chunk, k):
        peer = (own_z + k) % NZD
        return remote(
            total.at[chunk, (own_z + k) // NZD],
            line_in.at[chunk, own_z],
            line_send.at[chunk, peer],
            line_recv.at[chunk, own_z],
            at_line(peer),
        )

    def line_arrival(chunk, k):
        peer = (own_z + k) % NZD
        return remote(
            total.at[chunk, 0],
            line_in.at[chunk, peer],
            line_send.at[chunk, peer],
            line_recv.at[chunk, peer],
            at_line(peer),
        )

    def back_copy(chunk, peer, mine):
        return remote(
            back.at[chunk, peer],
            sums_hbm.at[chunk, mine],
            back_send.at[chunk, peer],
            back_recv.at[chunk, mine],
            at_group(peer),
        )

    def wait_x(parity, chunk, half, what):
        low, high = x_field(parity, chunk, half)
        if what == "recv":
            pl.when(has_low)(high.wait_recv)
            pl.when(has_high)(low.wait_recv)
        else:
            pl.when(has_low)(low.wait_send)
            pl.when(has_high)(high.wait_send)

    def wait_y(parity, half, what):
        low, high = y_field(parity, half)
        if what == "recv":
            pl.when(y_has_low)(high.wait_recv)
            pl.when(y_has_high)(low.wait_recv)
        else:
            pl.when(y_has_low)(low.wait_send)
            pl.when(y_has_high)(high.wait_send)

    def parts(parity, sent_at):
        return (0, 1) if sent_at == 0 else (None,)

    def send_halo(i, chunk, parity, half):
        low, high = x_field(parity, chunk, half)
        pl.when(has_low)(low.start)
        pl.when(has_high)(high.start)
        low, high = y_field(parity, half)

        @pl.when((i == 0) & y_has_low)
        def _():
            low.start()

        @pl.when((i == 1) & y_has_high)
        def _():
            high.start()

    def advance(t):
        now, later = t % 2, (t + 1) % 2

        def chunk_body(i, carry):
            chunk = order(i)
            for half in parts(now, t - 1):
                wait_x(now, chunk, half, "recv")
            if t >= 1:
                for half in parts(later, t - 2):
                    wait_x(later, chunk, half, "send")

            @pl.when(i == 0)
            def _():
                for half in parts(now, t - 1):
                    wait_y(now, half, "recv")
                if t >= 1:
                    for half in parts(later, t - 2):
                        wait_y(later, half, "send")

            base = pl.multiple_of(chunk * ROWS, ROWS)
            waves = field[now, 4:12, pl.ds(base + 8, ROWS), :].reshape(CX * ROWS, NZ)
            wave_high = waves.astype(jnp.bfloat16)
            wave_low = (waves - wave_high.astype(F32)).astype(jnp.bfloat16)
            depth[...] = (
                jnp.dot(wave_low, table_ref[0], preferred_element_type=F32)
                + jnp.dot(wave_high, table_ref[1], preferred_element_type=F32)
                + jnp.dot(wave_high, table_ref[0], preferred_element_type=F32)
            ).reshape(CX, ROWS, NZ)

            def row_body(j, carry):
                top = pl.multiple_of(base + j * 16, 16)
                up = [jnp.zeros((8, NZ), F32)] * 2
                down = [jnp.zeros((8, NZ), F32)] * 2
                for x in range(CX):
                    wave = forward[t, x, pl.ds(top, 16), :].astype(F32)
                    for half in range(2):
                        inner = pl.multiple_of(j * 16 + half * 8, 8)
                        row = pl.multiple_of(top + half * 8, 8)
                        r = pl.ds(pl.multiple_of(row + 8, 8), 8)
                        mid = field[now, 4 + x, r, :]
                        above = field[now, 4 + x, pl.ds(row, 8), :]
                        below = field[now, 4 + x, pl.ds(pl.multiple_of(row + 16, 8), 8), :]
                        total_sum = depth[x, pl.ds(inner, 8), :] + 3.0 * center_weight * mid
                        for k, w in enumerate(coefficients, 1):
                            paired = field[now, 4 + x + k, r, :] + field[now, 4 + x - k, r, :]
                            paired += pltpu.roll(jnp.where(eight >= k, mid, below), 8 - k, 0)
                            paired += pltpu.roll(jnp.where(eight < 8 - k, mid, above), k, 0)
                            total_sum += w * paired
                        out_rows = pl.ds(row, 8)
                        following = (
                            2.0 * mid
                            - field[later, 4 + x, r, :]
                            + courant[x, out_rows, :] * total_sum
                        )
                        if t > 0:
                            following = jnp.concatenate(
                                [
                                    following[:, :128]
                                    + jnp.where(
                                        at_depth,
                                        pltpu.roll(
                                            source[out_rows, :], (ZREC - t * CX - x) % 128, 1
                                        ),
                                        0.0,
                                    ),
                                    following[:, 128:],
                                ],
                                axis=1,
                            )
                        field[later, 4 + x, r, :] = following
                        value = wave[half * 8 : half * 8 + 8] * following
                        if t > 0:
                            value += image[x, out_rows, :]
                        image[x, out_rows, :] = value
                        if t == STEPS - 1:
                            up[half] = up[half] + rise[x] * value
                            down[half] = down[half] + fall[x] * value
                if t == STEPS - 1:
                    for half in range(2):
                        for side in range(2):
                            q = (i % GROUP) * (NQ // GROUP) + j * 4 + half * 2 + side
                            plane[i // GROUP, q, 0] = up[half][:, side * 128 : side * 128 + 128]
                            plane[i // GROUP, q, 1] = down[half][:, side * 128 : side * 128 + 128]
                return carry

            lax.fori_loop(0, ROWS // 16, row_body, 0)

            if t == 0:
                send_halo(i, chunk, later, 1)
                pl.when(i == PASS_AFTER)(pass_on)
            elif t < STEPS - 1:
                send_halo(i, chunk, later, None)
            else:
                batch = i // GROUP

                @pl.when(i % GROUP == GROUP - 1)
                def _():
                    for k in FAR_FIRST:
                        group_copy(batch, (own_q + k) % NQ, own_q).start()
                    group_in[batch, own_q] = plane[batch, own_q]

            return carry

        lax.fori_loop(0, CHUNKS, chunk_body, 0)

    advance(0)

    for k in range(1, NZD):
        peer = (own_z + k) % NZD
        pass_copy(peer, peer).wait_recv()
    arrived = landed[...].reshape(NG, 128)
    lane = iota((NG, 128), 1)
    spread = jnp.zeros((CY, 128), F32)
    for j in range(SLOTS):
        cell = arrived[:, 8 * j + STEPS : 8 * j + STEPS + 1].astype(jnp.int32)
        weights = jnp.zeros((NG, 128), F32)
        for t in range(STEPS):
            weights = jnp.where(lane // CX == t, arrived[:, 8 * j + t : 8 * j + t + 1], weights)
        weights = jnp.where(lane % CX == cell // CY, weights, 0.0)
        spot = jnp.where(lane == cell % CY, 1.0, 0.0)
        spread = spread + lax.dot_general(
            spot, weights, (((0,), (0,)), ((), ())), precision=HIGHEST, preferred_element_type=F32
        )
    source[...] = spread

    def inject(i, carry):
        chunk = order(i)
        out_rows = band_of(chunk, 0)
        in_rows = band_of(chunk, 8)
        packed_rows = source[out_rows, :]
        at_depth = iota((ROWS, 128), 1) == ZREC
        for x in range(CX):
            added = jnp.where(at_depth, pltpu.roll(packed_rows, (ZREC - x) % 128, 1), 0.0)
            wave = forward[0, x, out_rows, 0:128].astype(F32)
            field[1, 4 + x, in_rows, 0:128] += added
            image[x, out_rows, 0:128] += wave * added
        send_halo(i, chunk, 1, 0)
        return carry

    lax.fori_loop(0, CHUNKS, inject, 0)

    for t in range(1, STEPS):
        advance(t)

    store_last = pltpu.make_async_copy(
        field.at[STEPS % 2, pl.ds(4, CX), pl.ds(8, CY), :], last_hbm, store_sem.at[0]
    )
    store_image = pltpu.make_async_copy(image, image_hbm, store_sem.at[1])
    store_last.start()
    store_image.start()

    def reduce_group(batch, carry):
        for k in range(1, NQ):
            peer = (own_q + k) % NQ
            group_copy(batch, peer, peer).wait_recv()
        below_sum = group_in[batch, 0, 0]
        above_sum = group_in[batch, NQ - 1, 1]
        for q in range(1, NQ):
            below_sum = below_sum + group_in[batch, q, 0]
            above_sum = above_sum + group_in[batch, NQ - 1 - q, 1]
        total[batch, 0] = below_sum
        total[batch, 1] = above_sum
        for k in FAR_FIRST:
            line_copy(batch, k).start()
        line_in[batch, own_z] = jnp.zeros((8, 128), F32)
        return carry

    lax.fori_loop(0, BATCHES, reduce_group, 0)

    def return_sums(batch, carry):
        for k in range(1, NZD):
            line_arrival(batch, k).wait_recv()
        low_sum = jnp.zeros((8, 128), F32)
        high_sum = jnp.zeros((8, 128), F32)
        for z in range(NZD):
            part = line_in[batch, z]
            low_sum = low_sum + jnp.where(z < own_z, part, 0.0)
            high_sum = high_sum + jnp.where(z > own_z, part, 0.0)
        for q in range(NQ):
            back[batch, q, 0] = low_sum
            low_sum = low_sum + group_in[batch, q, 0]
            back[batch, NQ - 1 - q, 1] = high_sum
            high_sum = high_sum + group_in[batch, NQ - 1 - q, 1]
        for k in FAR_FIRST:
            back_copy(batch, (own_q + k) % NQ, own_q).start()
        pltpu.make_async_copy(
            back.at[batch, own_q], sums_hbm.at[batch, own_q], back_recv.at[batch, own_q]
        ).start()
        return carry

    lax.fori_loop(0, BATCHES, return_sums, 0)

    for k in range(1, NQ):
        peer = (own_q + k) % NQ
        pack_copy(peer, peer).wait_send()
    for k in range(1, NZD):
        peer = (own_z + k) % NZD
        pass_copy(peer, peer).wait_send()

    def wait_sends(i, carry):
        wait_x((STEPS - 1) % 2, i, None, "send")
        return carry

    lax.fori_loop(0, CHUNKS, wait_sends, 0)

    def wait_sums(i, carry):
        for k in range(1, NQ):
            peer = (own_q + k) % NQ
            group_copy(i, peer, peer).wait_send()
        for k in range(1, NZD):
            line_arrival(i, k).wait_send()
        return carry

    lax.fori_loop(0, BATCHES, wait_sums, 0)
    wait_y((STEPS - 1) % 2, None, "send")
    store_last.wait()
    store_image.wait()

    def finish(batch, carry):
        for k in range(1, NQ):
            peer = (own_q + k) % NQ
            back_copy(batch, peer, peer).wait()
        pltpu.make_async_copy(
            back.at[batch, own_q], sums_hbm.at[batch, own_q], back_recv.at[batch, own_q]
        ).wait()
        return carry

    lax.fori_loop(0, BATCHES, finish, 0)


def update_kernel(
    factor_ref,
    image_ref,
    sums_ref,
    last_ref,
    courant_ref,
    first_ref,
    second_ref,
    courant_out,
    first_out,
    second_out,
    last_out,
    fresh,
    store_sem,
):
    gx = lax.axis_index("gx")
    store_last = pltpu.make_async_copy(last_ref, last_out, store_sem.at[3, 0])
    store_last.start()
    rise = [factor_ref[gx * CX + x] for x in range(CX)]
    fall = [factor_ref[NG * CX + gx * CX + x] for x in range(CX)]

    def stores(part):
        band = pl.ds(part * UPDATE_ROWS, UPDATE_ROWS)
        return [
            pltpu.make_async_copy(fresh.at[k, :, band, :], out.at[:, band, :], store_sem.at[k, part])
            for k, out in enumerate((courant_out, first_out, second_out))
        ]

    for part in range(CY // UPDATE_ROWS):

        def body(j, carry):
            r = pl.ds(pl.multiple_of(part * UPDATE_ROWS + j * 8, 8), 8)
            row_tile = part * (UPDATE_ROWS // 8) + j
            turn = (CHUNKS - row_tile // (ROWS // 8)) % CHUNKS
            batch = turn // GROUP
            q = (turn % GROUP) * (NQ // GROUP) + 2 * (row_tile % (ROWS // 8))
            low, high = (
                jnp.concatenate([sums_ref[batch, q, k], sums_ref[batch, q + 1, k]], axis=1)
                for k in range(2)
            )
            values = [image_ref[x, r, :] for x in range(CX)]
            below = []
            for x in range(CX):
                low = low + rise[x] * values[x]
                below.append(low)
            for x in reversed(range(CX)):
                smoothed = fall[x] * below[x] + rise[x] * high
                high = high + fall[x] * values[x]
                first = beta_first * first_ref[x, r, :] + (1.0 - beta_first) * smoothed
                second = beta_second * second_ref[x, r, :] + (1.0 - beta_second) * smoothed * smoothed
                scaled = (1.0 / bias_second) * second
                root = scaled * lax.rsqrt(scaled)
                fresh[1, x, r, :] = first
                fresh[2, x, r, :] = second
                fresh[0, x, r, :] = courant_ref[x, r, :] - (learning_rate / bias_first) * first / (
                    root + epsilon
                )
            return carry

        lax.fori_loop(0, UPDATE_ROWS // 8, body, 0)
        for copy in stores(part):
            copy.start()
    for part in range(CY // UPDATE_ROWS):
        for copy in stores(part):
            copy.wait()
    store_last.wait()


def shards(
    courant,
    first_moment,
    second_moment,
    adjoint_prev,
    adjoint_now,
    forward_field,
    traces,
    trace_slab,
    trace_cell,
    trace_shot,
    rollback,
):
    factors = jnp.asarray(smoother_factors(NG * CX))
    table = depth_table()
    shape = jax.ShapeDtypeStruct((CX, CY, NZ), F32)
    anywhere = pl.BlockSpec(memory_space=pl.ANY)
    hbm = pl.BlockSpec(memory_space=pltpu.HBM)
    smem = pl.BlockSpec(memory_space=pltpu.SMEM)
    vmem = pl.BlockSpec(memory_space=pltpu.VMEM)
    dma = pltpu.SemaphoreType.DMA
    image, last, sums = pl.pallas_call(
        window_kernel,
        out_shape=(shape, shape, jax.ShapeDtypeStruct((BATCHES, NQ, 2, 8, 128), F32)),
        in_specs=[hbm] * 11,
        out_specs=(anywhere,) * 3,
        scratch_shapes=[
            pltpu.SMEM((SHOTS,), jnp.int32),
            pltpu.SMEM((2 * NG * CX,), F32),
            pltpu.VMEM((2, NZ, NZ), jnp.bfloat16),
            pltpu.VMEM((1, BLOCKS, 128), F32),
            pltpu.VMEM((1, BLOCKS), jnp.int32),
            pltpu.VMEM((1, BLOCKS), jnp.int32),
            pltpu.VMEM((1, BLOCKS), jnp.int32),
            pltpu.VMEM((2, CX + 8, CY + 16, NZ), F32),
            pltpu.VMEM((CX, CY, NZ), F32),
            pltpu.VMEM((STEPS, CX, CY, NZ), jnp.bfloat16),
            pltpu.VMEM((CX, CY, NZ), F32),
            pltpu.VMEM((CY, 128), F32),
            pltpu.VMEM((NQ, NZD, 1, 128), F32),
            pltpu.VMEM((NQ, NZD, 1, 128), F32),
            pltpu.VMEM((NZD, NQ, 1, 128), F32),
            pltpu.VMEM((CX, ROWS, NZ), F32),
            pltpu.VMEM((BATCHES, NQ, 2, 8, 128), F32),
            pltpu.VMEM((BATCHES, NQ, 2, 8, 128), F32),
            pltpu.VMEM((BATCHES, 2, 8, 128), F32),
            pltpu.VMEM((BATCHES, NZD, 8, 128), F32),
            pltpu.VMEM((BATCHES, NQ, 2, 8, 128), F32),
            dma((11,)),
            pltpu.SemaphoreType.REGULAR((2, 3)),
            dma((NQ,)),
            dma((NQ,)),
            dma((NZD,)),
            dma((NZD,)),
            dma((2, 2, CHUNKS)),
            dma((2, 2, CHUNKS)),
            dma((2, 2)),
            dma((2, 2)),
            dma((2, 2, CHUNKS)),
            dma((2, 2, CHUNKS)),
            dma((2, 2)),
            dma((2, 2)),
            dma((BATCHES, NQ)),
            dma((BATCHES, NQ)),
            dma((BATCHES, NZD)),
            dma((BATCHES, NZD)),
            dma((BATCHES, NQ)),
            dma((BATCHES, NQ)),
            dma((2,)),
        ],
        compiler_params=pltpu.CompilerParams(
            collective_id=0, has_side_effects=True, vmem_limit_bytes=24 << 20
        ),
    )(
        *(
            pltpu.with_memory_space_constraint(operand, pltpu.HBM)
            for operand in (
                rollback,
                factors,
                table,
                traces,
                trace_slab.reshape(1, BLOCKS),
                trace_cell,
                trace_shot,
                courant,
                adjoint_prev,
                adjoint_now,
                forward_field,
            )
        )
    )

    return pl.pallas_call(
        update_kernel,
        out_shape=(shape,) * 4,
        in_specs=[smem] + [vmem] * 6,
        out_specs=(anywhere,) * 4,
        scratch_shapes=[pltpu.VMEM((3, CX, CY, NZ), F32), dma((4, CY // UPDATE_ROWS))],
        compiler_params=pltpu.CompilerParams(vmem_limit_bytes=24 << 20),
    )(factors, image, sums, last, courant, first_moment, second_moment)


def solution(mesh):
    in_specs = (
        P("gx", "gy", None),
        P("gx", "gy", None),
        P("gx", "gy", None),
        P("gx", "gy", None),
        P("gx", "gy", None),
        P(None, "gx", "gy", None),
        P("gy", "gx", None),
        P("gy", "gx", None),
        P("gy", "gx"),
        P("gy", "gx"),
        P(),
    )
    out_specs = (P("gx", "gy", None),) * 4
    return jax.shard_map(shards, mesh=mesh, in_specs=in_specs, out_specs=out_specs, check_vma=False)
```

time: 65.5 us -> 63.3 us (0.966)
  Pallas kernels: 64.7 us -> 62.5 us
    pallas_call x1, Pallas kernels: 61.8 us -> 59.6 us  [shards(): pl.pallas_call(window_kernel, out_shape=(shape, shape, jax.ShapeDtypeStru...]
where the time goes in v3:
time: 63.3 us; the launch traced here: 63.2 us
  Pallas kernels  62.5 us (99%)
  between operations  0.71 us (1%)
    pallas_call x1, Pallas kernels, shards(): pl.pallas_call(window_kernel, out_shape=(shape, shape, jax.ShapeDtypeStru...  59.6 us
    pallas_call x1, Pallas kernels, shards(): pl.pallas_call(update_kernel, out_shape=(shape,) * 4, in_specs=[smem] + [...  2.88 us

profile of v3, /device:TPU:1, one launch (start us, length us, event | category | flops | bytes accessed | tf_op | source)
XLA Modules:
  0.0 63.2 jit_solution(14251283250783602175)
XLA Ops:
  0.6 0.0 copy-start
  0.6 0.0 copy-start.1
  0.7 0.0 copy-start.2
  0.7 0.0 copy-start.3
  0.7 59.6 %shard_map.156 = (f32[8,128,256]{2,1,0:T(8,128)S(1)}, f32[8,128,256]{2,1,0:T(8,128)S(1)}, f32[4,8,2,8,128]{4,3,2,1,0:T(8,128)S(1)}) custom-call(s32[16]{0:T(128)} %rollback_hbm.1, f32[1024]{0:T(1024)} %constant.4.clone.factor_hbm.factor_ref, bf16[2,256,256]{2,1,0:T(8,128)(2,1)} %constant.22.table_hbm, f32[1,128,128]{2,1,0:T(8,128)} %traces_hbm.1, ...), custom_call_target="tpu_custom_call" | custom-call | tf_op jit(solution)/shard_map/pallas_call | solution.py:776
  60.3 0.0 copy-done
  60.3 0.0 copy-done.1
  60.3 0.0 copy-done.2
  60.3 0.0 copy-done.3
  60.3 2.9 %shard_map.157 = (f32[8,128,256]{2,1,0:T(8,128)}, f32[8,128,256]{2,1,0:T(8,128)}, f32[8,128,256]{2,1,0:T(8,128)}, f32[8,128,256]{2,1,0:T(8,128)}) custom-call(f32[1024]{0:T(1024)S(1)} %copy-done.3, f32[8,128,256]{2,1,0:T(8,128)S(1)} %get-tuple-element.7.image_ref, f32[4,8,2,8,128]{4,3,2,1,0:T(8,128)S(1)} %get-tuple-element.8.sums_ref, ...), custom_call_target="tpu_custom_call" | custom-call | tf_op jit(solution)/shard_map/pallas_call | solution.py:847
Async XLA Ops:
  0.6 59.6 %copy-start = (f32[8,128,256]{2,1,0:T(8,128)S(1)}, f32[8,128,256]{2,1,0:T(8,128)}, u32[]{:S(2)}) copy-start(f32[8,128,256]{2,1,0:T(8,128)} %courant_ref.1) | copy-start | bytes 3145732
  0.6 59.6 %copy-start.1 = (f32[8,128,256]{2,1,0:T(8,128)S(1)}, f32[8,128,256]{2,1,0:T(8,128)}, u32[]{:S(2)}) copy-start(f32[8,128,256]{2,1,0:T(8,128)} %first_ref.1) | copy-start | bytes 3145732
  0.7 59.6 %copy-start.2 = (f32[8,128,256]{2,1,0:T(8,128)S(1)}, f32[8,128,256]{2,1,0:T(8,128)}, u32[]{:S(2)}) copy-start(f32[8,128,256]{2,1,0:T(8,128)} %second_ref.1) | copy-start | bytes 3145732
  0.7 59.6 %copy-start.3 = (f32[1024]{0:T(1024)S(1)}, f32[1024]{0:T(1024)}, u32[]{:S(2)}) copy-start(f32[1024]{0:T(1024)} %constant.4.clone.factor_hbm.factor_ref) | copy-start | bytes 12292

commit v4 on v3

--- a/solution.py
+++ b/solution.py
@@ -27,9 +27,9 @@
 CHUNKS = CY // ROWS
 GROUP = 32 // ROWS
 BATCHES = CHUNKS // GROUP
-PASS_AFTER = 2
+PASS_AFTER = 3
 FAR_FIRST = (4, 3, 5, 2, 6, 7, 1)
-UPDATE_ROWS = 32
+UPDATE_ROWS = 16
 
 coefficients = (8.0 / 5.0, -1.0 / 5.0, 8.0 / 315.0, -1.0 / 560.0)
 center_weight = -205.0 / 72.0
@@ -305,8 +305,6 @@
         pl.when(has_high)(high.start)
         return carry
 
-    send_now(0, 0)
-
     line_next = at_line((own_z + 1) % NZD)
     line_prev = at_line((own_z + NZD - 1) % NZD)
     signal(known_sem.at[0, 0], line_next)
@@ -353,7 +351,7 @@
 
     for k in FAR_FIRST:
         pack_copy((own_q + k) % NQ, own_q).start()
-    lax.fori_loop(1, CHUNKS, send_now, 0)
+    lax.fori_loop(0, CHUNKS, send_now, 0)
     passed[own_q] = packed[own_q]
 
     pl.semaphore_wait(known_sem.at[0, 0], 1)
@@ -602,8 +600,6 @@
         field.at[STEPS % 2, pl.ds(4, CX), pl.ds(8, CY), :], last_hbm, store_sem.at[0]
     )
     store_image = pltpu.make_async_copy(image, image_hbm, store_sem.at[1])
-    store_last.start()
-    store_image.start()
 
     def reduce_group(batch, carry):
         for k in range(1, NQ):
@@ -645,6 +641,8 @@
         return carry
 
     lax.fori_loop(0, BATCHES, return_sums, 0)
+    store_last.start()
+    store_image.start()
 
     for k in range(1, NQ):
         peer = (own_q + k) % NQ

time: 63.3 us -> 63 us (level)
  no operation moved by 1% of the time
where the time goes in v4:
time: 63 us; the launch traced here: 62.9 us
  Pallas kernels  62.1 us (99%)
  between operations  0.71 us (1%)
    pallas_call x1, Pallas kernels, shards(): pl.pallas_call(window_kernel, out_shape=(shape, shape, jax.ShapeDtypeStru...  59.3 us
    pallas_call x1, Pallas kernels, shards(): pl.pallas_call(update_kernel, out_shape=(shape,) * 4, in_specs=[smem] + [...  2.89 us

profile of v4, /device:TPU:1, one launch (start us, length us, event | category | flops | bytes accessed | tf_op | source)
XLA Modules:
  0.0 62.9 jit_solution(13710616816648824042)
XLA Ops:
  0.6 0.0 copy-start
  0.6 0.0 copy-start.1
  0.7 0.0 copy-start.2
  0.7 0.0 copy-start.3
  0.7 59.3 %shard_map.156 = (f32[8,128,256]{2,1,0:T(8,128)S(1)}, f32[8,128,256]{2,1,0:T(8,128)S(1)}, f32[4,8,2,8,128]{4,3,2,1,0:T(8,128)S(1)}) custom-call(s32[16]{0:T(128)} %rollback_hbm.1, f32[1024]{0:T(1024)} %constant.4.clone.factor_hbm.factor_ref, bf16[2,256,256]{2,1,0:T(8,128)(2,1)} %constant.22.table_hbm, f32[1,128,128]{2,1,0:T(8,128)} %traces_hbm.1, ...), custom_call_target="tpu_custom_call" | custom-call | tf_op jit(solution)/shard_map/pallas_call | solution.py:774
  59.9 0.0 copy-done
  60.0 0.0 copy-done.1
  60.0 0.0 copy-done.2
  60.0 0.0 copy-done.3
  60.0 2.9 %shard_map.157 = (f32[8,128,256]{2,1,0:T(8,128)}, f32[8,128,256]{2,1,0:T(8,128)}, f32[8,128,256]{2,1,0:T(8,128)}, f32[8,128,256]{2,1,0:T(8,128)}) custom-call(f32[1024]{0:T(1024)S(1)} %copy-done.3, f32[8,128,256]{2,1,0:T(8,128)S(1)} %get-tuple-element.7.image_ref, f32[4,8,2,8,128]{4,3,2,1,0:T(8,128)S(1)} %get-tuple-element.8.sums_ref, ...), custom_call_target="tpu_custom_call" | custom-call | tf_op jit(solution)/shard_map/pallas_call | solution.py:845
Async XLA Ops:
  0.6 59.3 %copy-start = (f32[8,128,256]{2,1,0:T(8,128)S(1)}, f32[8,128,256]{2,1,0:T(8,128)}, u32[]{:S(2)}) copy-start(f32[8,128,256]{2,1,0:T(8,128)} %courant_ref.1) | copy-start | bytes 3145732
  0.6 59.3 %copy-start.1 = (f32[8,128,256]{2,1,0:T(8,128)S(1)}, f32[8,128,256]{2,1,0:T(8,128)}, u32[]{:S(2)}) copy-start(f32[8,128,256]{2,1,0:T(8,128)} %first_ref.1) | copy-start | bytes 3145732
  0.7 59.3 %copy-start.2 = (f32[8,128,256]{2,1,0:T(8,128)S(1)}, f32[8,128,256]{2,1,0:T(8,128)}, u32[]{:S(2)}) copy-start(f32[8,128,256]{2,1,0:T(8,128)} %second_ref.1) | copy-start | bytes 3145732
  0.7 59.3 %copy-start.3 = (f32[1024]{0:T(1024)S(1)}, f32[1024]{0:T(1024)}, u32[]{:S(2)}) copy-start(f32[1024]{0:T(1024)} %constant.4.clone.factor_hbm.factor_ref) | copy-start | bytes 12292

commit v5 on v4

--- a/solution.py
+++ b/solution.py
@@ -210,106 +210,6 @@
     def _():
         field[:, 4:12, 8 + CY : 16 + CY, :] = jnp.zeros((2, CX, 8, NZ), F32)
 
-    pl.semaphore_wait(barrier, NQ - 1 + 4 + 1 - (own_q % (NQ - 1) + NQ - 2) // (NQ - 1))
-
-    has_low, has_high = gx > 0, gx < NG - 1
-    y_has_low, y_has_high = gy > 0, gy < NYD - 1
-    x_low = {"gx": (gx + NG - 1) % NG}
-    x_high = {"gx": (gx + 1) % NG}
-    y_low = {"gy": (gy + NYD - 1) % NYD}
-    y_high = {"gy": (gy + 1) % NYD}
-    every = pl.ds(0, NZ)
-
-    def order(i):
-        return (CHUNKS - i) % CHUNKS
-
-    def band_of(chunk, start):
-        return pl.ds(pl.multiple_of(start + chunk * ROWS, 8), ROWS)
-
-    def x_pair(parity, chunk, sources, lanes, send, recv):
-        band = band_of(chunk, 8)
-        low = remote(
-            sources[0], field.at[parity, pl.ds(12, 4), band, lanes], send(0), recv(1), x_low
-        )
-        high = remote(
-            sources[1], field.at[parity, pl.ds(0, 4), band, lanes], send(1), recv(0), x_high
-        )
-        return low, high
-
-    def x_field(parity, chunk, half=None):
-        band = band_of(chunk, 8)
-        if half is None:
-            lanes = every
-            send = lambda side: x_send.at[parity, side, chunk]
-            recv = lambda side: x_recv.at[parity, side, chunk]
-        else:
-            lanes = pl.ds(half * 128, 128)
-            send = lambda side: x_half_send.at[half, side, chunk]
-            recv = lambda side: x_half_recv.at[half, side, chunk]
-        sources = (
-            field.at[parity, pl.ds(4, 4), band, lanes],
-            field.at[parity, pl.ds(8, 4), band, lanes],
-        )
-        return x_pair(parity, chunk, sources, lanes, send, recv)
-
-    def y_pair(parity, sources, lanes, send, recv):
-        low = remote(
-            sources[0],
-            field.at[parity, pl.ds(4, CX), pl.ds(8 + CY, 8), lanes],
-            send(0),
-            recv(1),
-            y_low,
-        )
-        high = remote(
-            sources[1], field.at[parity, pl.ds(4, CX), pl.ds(0, 8), lanes], send(1), recv(0), y_high
-        )
-        return low, high
-
-    def y_field(parity, half=None):
-        if half is None:
-            lanes = every
-            send = lambda side: y_send.at[parity, side]
-            recv = lambda side: y_recv.at[parity, side]
-        else:
-            lanes = pl.ds(half * 128, 128)
-            send = lambda side: y_half_send.at[half, side]
-            recv = lambda side: y_half_recv.at[half, side]
-        sources = (
-            field.at[parity, pl.ds(4, CX), pl.ds(8, 8), lanes],
-            field.at[parity, pl.ds(4, CX), pl.ds(CY, 8), lanes],
-        )
-        return y_pair(parity, sources, lanes, send, recv)
-
-    low, high = y_pair(
-        0,
-        (now_hbm.at[:, pl.ds(0, 8), :], now_hbm.at[:, pl.ds(CY - 8, 8), :]),
-        every,
-        lambda side: y_send.at[0, side],
-        lambda side: y_recv.at[0, side],
-    )
-    pl.when(y_has_low)(low.start)
-    pl.when(y_has_high)(high.start)
-
-    def send_now(i, carry):
-        chunk = order(i)
-        band = band_of(chunk, 0)
-        low, high = x_pair(
-            0,
-            chunk,
-            (now_hbm.at[pl.ds(0, 4), band, :], now_hbm.at[pl.ds(4, 4), band, :]),
-            every,
-            lambda side: x_send.at[0, side, chunk],
-            lambda side: x_recv.at[0, side, chunk],
-        )
-        pl.when(has_low)(low.start)
-        pl.when(has_high)(high.start)
-        return carry
-
-    line_next = at_line((own_z + 1) % NZD)
-    line_prev = at_line((own_z + NZD - 1) % NZD)
-    signal(known_sem.at[0, 0], line_next)
-    signal(known_sem.at[1, 0], line_prev)
-
     for copy in small[:5]:
         copy.wait()
     rows = iota((BLOCKS, 128), 0)
@@ -338,6 +238,106 @@
     packed[...] = jnp.dot(
         named, entries, precision=HIGHEST, preferred_element_type=F32
     ).reshape(NQ, NZD, 1, 128)
+
+    pl.semaphore_wait(barrier, NQ - 1 + 4 + 1 - (own_q % (NQ - 1) + NQ - 2) // (NQ - 1))
+
+    has_low, has_high = gx > 0, gx < NG - 1
+    y_has_low, y_has_high = gy > 0, gy < NYD - 1
+    x_low = {"gx": (gx + NG - 1) % NG}
+    x_high = {"gx": (gx + 1) % NG}
+    y_low = {"gy": (gy + NYD - 1) % NYD}
+    y_high = {"gy": (gy + 1) % NYD}
+    every = pl.ds(0, NZ)
+
+    def order(i):
+        return (CHUNKS - i) % CHUNKS
+
+    def band_of(chunk, start):
+        return pl.ds(pl.multiple_of(start + chunk * ROWS, 8), ROWS)
+
+    def x_pair(parity, chunk, sources, lanes, send, recv):
+        band = band_of(chunk, 8)
+        low = remote(
+            sources[0], field.at[parity, pl.ds(12, 4), band, lanes], send(0), recv(1), x_low
+        )
+        high = remote(
+            sources[1], field.at[parity, pl.ds(0, 4), band, lanes], send(1), recv(0), x_high
+        )
+        return low, high
+
+    def x_field(parity, chunk, half=None):
+        band = band_of(chunk, 8)
+        if half is None:
+            lanes = every
+            send = lambda side: x_send.at[parity, side, chunk]
+            recv = lambda side: x_recv.at[parity, side, chunk]
+        else:
+            lanes = pl.ds(half * 128, 128)
+            send = lambda side: x_half_send.at[half, side, chunk]
+            recv = lambda side: x_half_recv.at[half, side, chunk]
+        sources = (
+            field.at[parity, pl.ds(4, 4), band, lanes],
+            field.at[parity, pl.ds(8, 4), band, lanes],
+        )
+        return x_pair(parity, chunk, sources, lanes, send, recv)
+
+    def y_pair(parity, sources, lanes, send, recv):
+        low = remote(
+            sources[0],
+            field.at[parity, pl.ds(4, CX), pl.ds(8 + CY, 8), lanes],
+            send(0),
+            recv(1),
+            y_low,
+        )
+        high = remote(
+            sources[1], field.at[parity, pl.ds(4, CX), pl.ds(0, 8), lanes], send(1), recv(0), y_high
+        )
+        return low, high
+
+    def y_field(parity, half=None):
+        if half is None:
+            lanes = every
+            send = lambda side: y_send.at[parity, side]
+            recv = lambda side: y_recv.at[parity, side]
+        else:
+            lanes = pl.ds(half * 128, 128)
+            send = lambda side: y_half_send.at[half, side]
+            recv = lambda side: y_half_recv.at[half, side]
+        sources = (
+            field.at[parity, pl.ds(4, CX), pl.ds(8, 8), lanes],
+            field.at[parity, pl.ds(4, CX), pl.ds(CY, 8), lanes],
+        )
+        return y_pair(parity, sources, lanes, send, recv)
+
+    low, high = y_pair(
+        0,
+        (now_hbm.at[:, pl.ds(0, 8), :], now_hbm.at[:, pl.ds(CY - 8, 8), :]),
+        every,
+        lambda side: y_send.at[0, side],
+        lambda side: y_recv.at[0, side],
+    )
+    pl.when(y_has_low)(low.start)
+    pl.when(y_has_high)(high.start)
+
+    def send_now(i, carry):
+        chunk = order(i)
+        band = band_of(chunk, 0)
+        low, high = x_pair(
+            0,
+            chunk,
+            (now_hbm.at[pl.ds(0, 4), band, :], now_hbm.at[pl.ds(4, 4), band, :]),
+            every,
+            lambda side: x_send.at[0, side, chunk],
+            lambda side: x_recv.at[0, side, chunk],
+        )
+        pl.when(has_low)(low.start)
+        pl.when(has_high)(high.start)
+        return carry
+
+    line_next = at_line((own_z + 1) % NZD)
+    line_prev = at_line((own_z + NZD - 1) % NZD)
+    signal(known_sem.at[0, 0], line_next)
+    signal(known_sem.at[1, 0], line_prev)
 
     def pack_copy(peer, mine):
         return remote(

time: 63 us -> 62.4 us (level)
  no operation moved by 1% of the time
where the time goes in v5:
time: 62.4 us; the launch traced here: 62.3 us
  Pallas kernels  61.6 us (99%)
  between operations  0.71 us (1%)
    pallas_call x1, Pallas kernels, shards(): pl.pallas_call(window_kernel, out_shape=(shape, shape, jax.ShapeDtypeStru...  58.7 us
    pallas_call x1, Pallas kernels, shards(): pl.pallas_call(update_kernel, out_shape=(shape,) * 4, in_specs=[smem] + [...  2.89 us

profile of v5, /device:TPU:1, one launch (start us, length us, event | category | flops | bytes accessed | tf_op | source)
XLA Modules:
  0.0 62.3 jit_solution(3882270606608229943)
XLA Ops:
  0.6 0.0 copy-start
  0.6 0.0 copy-start.1
  0.7 0.0 copy-start.2
  0.7 0.0 copy-start.3
  0.7 58.7 %shard_map.156 = (f32[8,128,256]{2,1,0:T(8,128)S(1)}, f32[8,128,256]{2,1,0:T(8,128)S(1)}, f32[4,8,2,8,128]{4,3,2,1,0:T(8,128)S(1)}) custom-call(s32[16]{0:T(128)} %rollback_hbm.1, f32[1024]{0:T(1024)} %constant.4.clone.factor_hbm.factor_ref, bf16[2,256,256]{2,1,0:T(8,128)(2,1)} %constant.22.table_hbm, f32[1,128,128]{2,1,0:T(8,128)} %traces_hbm.1, ...), custom_call_target="tpu_custom_call" | custom-call | tf_op jit(solution)/shard_map/pallas_call | solution.py:774
  59.4 0.0 copy-done
  59.4 0.0 copy-done.1
  59.4 0.0 copy-done.2
  59.4 0.0 copy-done.3
  59.5 2.9 %shard_map.157 = (f32[8,128,256]{2,1,0:T(8,128)}, f32[8,128,256]{2,1,0:T(8,128)}, f32[8,128,256]{2,1,0:T(8,128)}, f32[8,128,256]{2,1,0:T(8,128)}) custom-call(f32[1024]{0:T(1024)S(1)} %copy-done.3, f32[8,128,256]{2,1,0:T(8,128)S(1)} %get-tuple-element.7.image_ref, f32[4,8,2,8,128]{4,3,2,1,0:T(8,128)S(1)} %get-tuple-element.8.sums_ref, ...), custom_call_target="tpu_custom_call" | custom-call | tf_op jit(solution)/shard_map/pallas_call | solution.py:845
Async XLA Ops:
  0.6 58.8 %copy-start = (f32[8,128,256]{2,1,0:T(8,128)S(1)}, f32[8,128,256]{2,1,0:T(8,128)}, u32[]{:S(2)}) copy-start(f32[8,128,256]{2,1,0:T(8,128)} %courant_ref.1) | copy-start | bytes 3145732
  0.6 58.8 %copy-start.1 = (f32[8,128,256]{2,1,0:T(8,128)S(1)}, f32[8,128,256]{2,1,0:T(8,128)}, u32[]{:S(2)}) copy-start(f32[8,128,256]{2,1,0:T(8,128)} %first_ref.1) | copy-start | bytes 3145732
  0.7 58.8 %copy-start.2 = (f32[8,128,256]{2,1,0:T(8,128)S(1)}, f32[8,128,256]{2,1,0:T(8,128)}, u32[]{:S(2)}) copy-start(f32[8,128,256]{2,1,0:T(8,128)} %second_ref.1) | copy-start | bytes 3145732
  0.7 58.8 %copy-start.3 = (f32[1024]{0:T(1024)S(1)}, f32[1024]{0:T(1024)}, u32[]{:S(2)}) copy-start(f32[1024]{0:T(1024)} %constant.4.clone.factor_hbm.factor_ref) | copy-start | bytes 12292
